TPU v7x, 32 devices: a whole 2x2x4 slice. The times are simulated.
32 devices in a mesh: chan: 4 (over y, core), seq: 8 (over z, x).
Axes of the slice: x: 2, y: 2, z: 4, core: 2. Of those that a mesh axis runs over, the one named last changes fastest.
Arguments:
- query_proj: bfloat16 [65536, 2048], P('seq', 'chan'), may hold values from -6 to 6
- key_proj: bfloat16 [65536, 2048], P('seq', 'chan'), may hold values from -6 to 6
- value_proj: bfloat16 [65536, 2048], P('seq', 'chan'), may hold values from -6 to 6
- short_taps: float32 [3, 3, 2048], P(None, None, 'chan'), may hold values from -3.5 to 3.5
- skip_gain: float32 [2048], P('chan'), may hold values from -6 to 6
- long_filter: float32 [4, 65536], P('chan', 'seq'), may hold values from -0.0234375 to 0.0234375
Outputs:
- mixed: float32 [65536, 2048], P('seq', 'chan')
All inputs are finite; a program needn't handle non-finite values.
Results may differ from a plain program's by a relative error of at most 0.0003.
Values may be sent and summed in bfloat16 or wider, within the bound.
No kernel may reach another device: no remote copies, remote signals or barrier semaphores. Data moves between devices by JAX's collectives and lax.ppermute only.
A program may use at most 256 MiB of HBM per device.

v0:
```python
from functools import partial
import math

import jax
import jax.numpy as jnp
from jax import lax
from jax.sharding import PartitionSpec as P

A = 256
B = 256


EXACT = lax.Precision.HIGHEST


def from_behind(value, axis, steps):
    count = lax.axis_size(axis)
    initial, last = (max(0, -steps), min(count, count - steps))
    return lax.ppermute(value, axis, [(source, source + steps) for source in range(initial, last)])


def phase_table(count_rows, count_cols, period, col_start):
    row_index = lax.broadcasted_iota(jnp.int32, (count_rows, count_cols), 0)
    col_index = lax.broadcasted_iota(jnp.int32, (count_rows, count_cols), 1) + col_start
    residue = row_index * col_index % period
    angle_val = 2.0 * math.pi / period * residue.astype(jnp.float32)
    return (jnp.cos(angle_val), jnp.sin(angle_val))


def complex_apply(pattern, matrix_re, matrix_im, data_re, data_im):
    product = partial(jnp.einsum, pattern, precision=EXACT)
    if data_im is None:
        return (product(matrix_re, data_re), product(matrix_im, data_re))
    return (
        product(matrix_re, data_re) - product(matrix_im, data_im),
        product(matrix_re, data_im) + product(matrix_im, data_re),
    )


def complex_times(first_re, first_im, second_re, second_im):
    return (
        first_re * second_re - first_im * second_im,
        first_re * second_im + first_im * second_re,
    )


def lane_forward(block, twiddle_re, twiddle_im):
    cos_b, sin_b = phase_table(B, B, B, 0)
    inner_re, inner_im = complex_apply("kb,bam->kam", cos_b, -sin_b, block[:, :, 0], block[:, :, 1])
    return complex_times(inner_re, inner_im, twiddle_re[:, :, None], -twiddle_im[:, :, None])


def lane_spectrum(block):
    cos_a, sin_a = phase_table(A, A, A, 0)
    return complex_apply("ja,kam->kjm", cos_a, -sin_a, block[:, :, 0], block[:, :, 1])


def lane_unspectrum(spec_re, spec_im):
    cos_a, sin_a = phase_table(A, A, A, 0)
    return complex_apply("ja,kjm->kam", cos_a, sin_a, spec_re, spec_im)


def lane_backward(block, twiddle_re, twiddle_im):
    turned_re, turned_im = complex_times(
        block[:, :, 0], block[:, :, 1], twiddle_re[:, :, None], twiddle_im[:, :, None]
    )
    cos_b, sin_b = phase_table(B, B, B, 0)
    out_re, out_im = complex_apply("kb,kam->bam", cos_b, sin_b, turned_re, turned_im)
    factor = 1.0 / (A * B)
    return (out_re * factor, out_im * factor)


def per_device(query_proj, key_proj, value_proj, short_taps, skip_gain, long_filter):
    tok_count, chan_width = query_proj.shape
    previous = from_behind((query_proj[-2:], key_proj[-2:], value_proj[-2:]), "seq", 1)

    def depthwise(signal, before, column):
        padded = jnp.concatenate([before, signal], axis=0).astype(jnp.float32)
        return (
            short_taps[0, column] * padded[2:]
            + short_taps[1, column] * padded[1:-1]
            + short_taps[2, column] * padded[:-2]
        )

    query_short = depthwise(query_proj, previous[0], 0)
    key_short = depthwise(key_proj, previous[1], 1)
    value_short = depthwise(value_proj, previous[2], 2)
    gated = key_short * value_short
    seq_count = lax.axis_size("seq")
    low_count = A // seq_count
    high_count = tok_count // A
    half_width = chan_width // 2
    signal_block = gated.reshape(high_count, A, 2, half_width)
    filter_taps_local = long_filter.reshape(high_count, A, 1, 1)
    filter_block = jnp.concatenate([filter_taps_local, jnp.zeros_like(filter_taps_local)], axis=2)
    signal_block, filter_block = (
        lax.all_to_all(signal_block, "seq", split_axis=1, concat_axis=0, tiled=True),
        lax.all_to_all(filter_block, "seq", split_axis=1, concat_axis=0, tiled=True),
    )
    position = lax.axis_index("seq")
    twiddle_re, twiddle_im = phase_table(B, low_count, A * B, position * low_count)
    sig_re, sig_im = lane_forward(signal_block, twiddle_re, twiddle_im)
    fil_re, fil_im = lane_forward(filter_block, twiddle_re, twiddle_im)
    signal_block, filter_block = (
        lax.all_to_all(
            jnp.stack([sig_re, sig_im], axis=2), "seq", split_axis=0, concat_axis=1, tiled=True
        ),
        lax.all_to_all(
            jnp.stack([fil_re, fil_im], axis=2), "seq", split_axis=0, concat_axis=1, tiled=True
        ),
    )
    freq_re, freq_im = lane_spectrum(signal_block)
    spectrum_re, spectrum_im = lane_spectrum(filter_block)
    mult_re, mult_im = complex_times(freq_re, freq_im, spectrum_re, spectrum_im)
    back_re, back_im = lane_unspectrum(mult_re, mult_im)
    back_block = lax.all_to_all(
        jnp.stack([back_re, back_im], axis=2), "seq", split_axis=1, concat_axis=0, tiled=True
    )
    conv_re, conv_im = lane_backward(back_block, twiddle_re, twiddle_im)
    convolved = lax.all_to_all(
        jnp.stack([conv_re, conv_im], axis=2), "seq", split_axis=0, concat_axis=1, tiled=True
    )
    convolved = convolved.reshape(tok_count, chan_width)
    return query_short * (convolved + skip_gain * gated)


def solution(mesh):
    return jax.shard_map(
        per_device,
        mesh=mesh,
        in_specs=(
            P("seq", "chan"),
            P("seq", "chan"),
            P("seq", "chan"),
            P(None, None, "chan"),
            P("chan"),
            P("chan", "seq"),
        ),
        out_specs=P("seq", "chan"),
        check_vma=False,
    )
```

profile of v0, /device:TPU:0, one launch (start us, length us, event | category | flops | bytes accessed | tf_op | source)
XLA Modules:
  0.0 1994.9 jit_solution(7467788233628211995)
XLA Ops:
  34.6 39.5 %fusion.1 = f32[8192,512]{1,0:T(8,128)} fusion(f32[8194,512]{1,0:T(8,128)} %maximum_convert_fusion.2, f32[8194,512]{1,0:T(8,128)} %maximum_convert_fusion.1, f32[512]{0:T(512)S(1)} %bitcast.234, f32[512]{0:T(512)S(1)} %bitcast.235, f32[512]{0:T(512)S(1)} %bitcast.230, f32[512]{0:T(512)S(1)} %bitcast.231, f32[512]{0:T(512)S(1)} %bitcast.232, f32[512]{0:T(512)S(1)} %bitcast.233), kind=kLoop, calls=%fused_computation.2 | loop fusion | flops 46137344 | bytes 117452800 | tf_op jit(solution)/shard_map/mul | solution.py:88
  74.1 19.9 reshape.143
  94.0 17.7 copy.125
  128.2 351.8 %all-to-all-done = f32[32,256,2,256]{3,0,2,1:T(8,128)} async-done(((f32[32,256,2,256]{3,0,2,1:T(8,128)}), f32[32,256,2,256]{3,0,2,1:T(8,128)}, u32[]{:S(2)}, u32[]{:S(2)}) %all-to-all-start) | async-done | bytes 16777248 | tf_op jit(solution)/shard_map/all_to_all | solution.py:97
  513.9 11.8 fusion.19
  525.8 21.5 %subtract_bitcast_fusion.1 = (f32[256,32,1,256]{3,0,1,2:T(8,128)}, f32[256,32,1,256]{3,0,1,2:T(8,128)}) fusion(f32[256,32]{0,1:T(8,128)S(1)} %get-tuple-element.21, f32[256,32]{0,1:T(8,128)S(1)} %get-tuple-element.24, f32[256,32,256]{2,0,1:T(8,128)} %fusion.16, f32[256,32,256]{2,0,1:T(8,128)} %fusion.17, f32[256,32,256]{2,0,1:T(8,128)} %fusion.19, ...), kind=kOutput, calls=%fused_computation.46 | convolution fusion | flops 6460145664 | bytes 50397184 | tf_op jit(solution)/shard_map/kb,bam->kam/dot_general | solution.py:36
  554.2 20.2 %copy.132 = f32[256,32,2,256]{3,1,2,0:T(8,128)} copy(f32[256,32,2,256]{3,0,1,2:T(8,128)S(1)} %pad_maximum_fusion) | data formatting | bytes 33554432 | tf_op jit(solution)/shard_map/stack | solution.py:106
  587.0 356.3 %all-to-all-done.1 = f32[256,32,2,256]{3,1,2,0:T(8,128)} async-done(((f32[256,32,2,256]{3,1,2,0:T(8,128)}), f32[256,32,2,256]{3,1,2,0:T(8,128)}, u32[]{:S(2)}, u32[]{:S(2)}) %all-to-all-start.1) | async-done | bytes 16777248 | tf_op jit(solution)/shard_map/all_to_all | solution.py:105
  949.8 18.3 fusion.20
  968.1 18.0 fusion.21
  986.1 18.1 fusion.23
  1004.2 25.9 %multiply_subtract_fusion.1 = (f32[32,256,256]{2,1,0:T(8,128)}, f32[32,256,256]{2,1,0:T(8,128)}) fusion(f32[32,256]{1,0:T(8,128)S(1)} %convolution_add_fusion, f32[32,256]{1,0:T(8,128)S(1)} %convolution_subtract_fusion, f32[32,256,256]{2,1,0:T(8,128)} %fusion.20, f32[32,256,256]{2,1,0:T(8,128)} %fusion.21, f32[32,256,256]{2,1,0:T(8,128)} %fusion.23, ...), kind=kOutput, calls=%fused_computation.44 | convolution fusion | flops 6460145664 | bytes 50397184 | tf_op jit(solution)/shard_map/ja,kam->kjm/dot_general | solution.py:36
  1030.2 13.4 fusion.10
  1083.2 19.9 copy.149
  1103.1 367.2 %all_to_all.105 = f32[32,256,2,256]{3,0,2,1:T(8,128)S(1)} all-to-all(f32[32,256,2,256]{3,0,2,1:T(8,128)} %copy.149), channel_id=1, replica_groups=mesh['chan'=4,'seq'=8] {'seq'}, dimensions={1} | all-to-all | bytes 33554432 | tf_op jit(solution)/shard_map/all_to_all | solution.py:116
  1472.4 12.4 fusion.28
  1484.8 12.6 fusion.29
  1497.5 17.5 multiply_bitcast_fusion.1
  1515.0 16.1 multiply_bitcast_fusion
  1537.9 20.3 %copy.152 = f32[256,32,2,256]{3,1,2,0:T(8,128)} copy(f32[256,32,2,256]{3,0,1,2:T(8,128)S(1)} %pad_maximum_fusion.2) | data formatting | bytes 33554432 | tf_op jit(solution)/shard_map/stack | solution.py:121
  1568.5 129.9 %collective-permute-done = bf16[2,512]{1,0:T(2,128)(2,1)S(1)} collective-permute-done((bf16[2,512]{1,0:T(2,128)(2,1)S(1)}, bf16[2,512]{1,0:T(2,128)(2,1)S(1)}, u32[]{:S(2)}, u32[]{:S(2)}) %collective-permute-start) | collective-permute-done | bytes 2080 | tf_op jit(solution)/shard_map/ppermute | solution.py:19
  1708.2 217.7 %all-to-all-done.5 = f32[256,32,2,256]{3,1,2,0:T(8,128)} async-done(((f32[256,32,2,256]{3,1,2,0:T(8,128)}), f32[256,32,2,256]{3,1,2,0:T(8,128)}, u32[]{:S(2)}, u32[]{:S(2)}) %all-to-all-start.5) | async-done | bytes 16777248 | tf_op jit(solution)/shard_map/all_to_all | solution.py:120
  1925.9 27.6 %copy.153 = f32[32,8,32,2,256]{4,3,2,1,0:T(2,128)S(1)} copy(f32[32,8,32,2,256]{4,2,3,0,1:T(8,128)} %bitcast.62) | data formatting | bytes 33554432 | tf_op jit(solution)/shard_map/all_to_all | solution.py:120
  1960.8 33.7 %fusion.6 = f32[8192,512]{1,0:T(8,128)} fusion(f32[8194,512]{1,0:T(8,128)} %maximum_convert_fusion, f32[8192,512]{1,0:T(8,128)} %bitcast.215, f32[8192,512]{1,0:T(8,128)} %fusion.1, f32[512]{0:T(512)S(1)} %copy-done.9, f32[512]{0:T(512)S(1)} %bitcast.228, f32[512]{0:T(512)S(1)} %bitcast.229, f32[512]{0:T(512)S(1)} %bitcast.227), kind=kLoop, calls=%fused_computation.13 | loop fusion | flops 33554432 | bytes 100671488 | tf_op jit(solution)/shard_map/mul | solution.py:124
  (87 shorter events, 186.7 us)
Async XLA Ops:
  0.7 17.3 collective-permute-start.1
  6.2 22.1 %collective-permute-start.2 = (bf16[2,512]{1,0:T(2,128)(2,1)S(1)}, bf16[2,512]{1,0:T(2,128)(2,1)S(1)}, u32[]{:S(2)}, u32[]{:S(2)}) collective-permute-start(bf16[2,512]{1,0:T(2,128)(2,1)S(1)} %slice.108), channel_id=1, source_target_pairs={{0,1},{1,2},{2,3},{3,4},{4,5},{5,6},{6,7},{8,9},{9,10},{10,11},{11... | collective-permute-start | bytes 6152 | tf_op jit(solution)/shard_map/ppermute | solution.py:19
  11.6 100.1 %all-to-all-start.2 = ((f32[8,1,2048]{2,1,0:T(1,128)}), f32[8,1,2048]{2,1,0:T(1,128)S(1)}, u32[]{:S(2)}, u32[]{:S(2)}) async-start(f32[8,1,2048]{2,1,0:T(1,128)} %reshape.153), calls=%async_computation.2 | async-start | bytes 131072 | tf_op jit(solution)/shard_map/all_to_all | solution.py:98
  16.4 11.9 slice-start.2
  18.0 10.4 slice-start.3
  111.7 368.3 %all-to-all-start = ((f32[32,256,2,256]{3,0,2,1:T(8,128)}), f32[32,256,2,256]{3,0,2,1:T(8,128)}, u32[]{:S(2)}, u32[]{:S(2)}) async-start(f32[32,256,2,256]{3,0,2,1:T(8,128)} %copy.125), calls=%async_computation | async-start | bytes 33554432 | tf_op jit(solution)/shard_map/all_to_all | solution.py:97
  480.0 94.5 %all-to-all-start.3 = ((f32[8,1,2048]{2,1,0:T(1,128)}), f32[8,1,2048]{2,1,0:T(1,128)S(1)}, u32[]{:S(2)}, u32[]{:S(2)}) async-start(f32[8,1,2048]{2,1,0:T(1,128)} %reshape.155), calls=%async_computation.3 | async-start | bytes 131072 | tf_op jit(solution)/shard_map/all_to_all | solution.py:108
  490.6 23.3 %copy-start.2 = (f32[8,32,32,2,256]{4,1,0,2,3:T(8,128)}, f32[8,32,32,2,256]{4,1,0,2,3:T(8,128)S(1)}, u32[]{:S(2)}) copy-start(f32[8,32,32,2,256]{4,1,0,2,3:T(8,128)S(1)} %copy.127) | copy-start | bytes 50331652
  574.4 368.8 %all-to-all-start.1 = ((f32[256,32,2,256]{3,1,2,0:T(8,128)}), f32[256,32,2,256]{3,1,2,0:T(8,128)}, u32[]{:S(2)}, u32[]{:S(2)}) async-start(f32[256,32,2,256]{3,1,2,0:T(8,128)} %copy.132), calls=%async_computation.1 | async-start | bytes 33554432 | tf_op jit(solution)/shard_map/all_to_all | solution.py:105
  949.8 36.3 %copy-start.1 = (f32[32,8,32,2,256]{4,2,1,3,0:T(8,128)}, f32[32,8,32,2,256]{4,2,1,3,0:T(8,128)S(1)}, u32[]{:S(2)}) copy-start(f32[32,8,32,2,256]{4,2,1,3,0:T(8,128)S(1)} %copy.133) | copy-start | bytes 50331652
  1030.1 13.4 copy-start.3
  1030.1 21.1 %slice-start = ((s8[8388608]{0:T(1024)(128)(4,1)}), s8[4194304]{0:T(1024)(128)(4,1)S(1)}, s32[]{:S(2)}) async-start(s8[8388608]{0:T(1024)(128)(4,1)} %bitcast.213), calls=%async_computation.6 | async-start | bytes 8388608
  1043.5 7.7 slice-start.1
  1470.3 2.1 copy-start.5
  1472.4 12.5 copy-start
  1497.5 17.5 copy-start.4
  1558.3 367.6 %all-to-all-start.5 = ((f32[256,32,2,256]{3,1,2,0:T(8,128)}), f32[256,32,2,256]{3,1,2,0:T(8,128)}, u32[]{:S(2)}, u32[]{:S(2)}) async-start(f32[256,32,2,256]{3,1,2,0:T(8,128)} %copy.152), calls=%async_computation.5 | async-start | bytes 33554432 | tf_op jit(solution)/shard_map/all_to_all | solution.py:120
  1564.7 133.7 %collective-permute-start = (bf16[2,512]{1,0:T(2,128)(2,1)S(1)}, bf16[2,512]{1,0:T(2,128)(2,1)S(1)}, u32[]{:S(2)}, u32[]{:S(2)}) collective-permute-start(bf16[2,512]{1,0:T(2,128)(2,1)S(1)} %slice.94), channel_id=1, source_target_pairs={{0,1},{1,2},{2,3},{3,4},{4,5},{5,6},{6,7},{8,9},{9,10},{10,11},{11... | collective-permute-start | bytes 6152 | tf_op jit(solution)/shard_map/ppermute | solution.py:19
  1953.5 7.3 copy-start.6
  1953.5 7.3 copy-start.7
  1953.5 7.3 copy-start.8
  1953.5 7.3 copy-start.9
where the time goes:
time: 2010 us; the launch traced here: 1990 us
  waiting for transfers between devices  1060 us (53%)
  blocking collectives  367 us (18%)
  matrix products  249 us (12%)
  local copies, waits for them, and re-layouts  157 us (8%)
  other arithmetic  126 us (6%)
  starting transfers between devices  38.8 us (2%)
    all_to_all x1, blocking collectives, per_device(): lax.all_to_all(jnp.stack([back_re, back_im], axis=2), 'seq', split_axis=1...  367 us
    all_to_all x1, waiting for transfers between devices, per_device(): lax.all_to_all(jnp.stack([sig_re, sig_im], axis=2), 'seq', split_axis=0,...  356 us
    all_to_all x1, waiting for transfers between devices, per_device(): lax.all_to_all(signal_block, 'seq', split_axis=1, concat_axis=0, tiled=True)  352 us
    all_to_all x1, waiting for transfers between devices, per_device(): lax.all_to_all(jnp.stack([conv_re, conv_im], axis=2), 'seq', split_axis=0...  218 us
    ppermute x3, waiting for transfers between devices, from_behind(): lax.ppermute(value, axis, [(source, source + steps) for source in range(i...  130 us
    dot_general x6, matrix products, complex_apply(): product(matrix_re, data_im) + product(matrix_im, data_re)  70.2 us
    dot_general x6, matrix products, complex_apply(): product(matrix_im, data_im)  64 us
    dot_general x6, matrix products, complex_apply(): product(matrix_im, data_re)  59.5 us
  transfers between devices with their start and end apart: 8, of which 4 were waited for; matrix products, arithmetic and copies ran while one was open for 11% of the time, Pallas kernels for 0%

commit v1 on v0

v1 whole, which is shorter than its diff:
```python
from functools import partial

import jax
import jax.numpy as jnp
import numpy as np
from jax import lax
from jax.experimental import pallas as pl
from jax.experimental.pallas import tpu as pltpu
from jax.sharding import PartitionSpec as P

A = 256
B = 256
LANES = 128

POWER = 15
TOP = 2.0**8.375
LEAST = 1e-34


def tables():
    index = np.arange(A)
    angle = 2.0 * np.pi / A * (np.outer(index, index) % A)
    cos, sin = np.cos(angle), -np.sin(angle)
    bf16 = jnp.bfloat16
    cos_hi, sin_hi = cos.astype(bf16), sin.astype(bf16)
    cos_lo = (cos - cos_hi.astype(np.float64)).astype(bf16)
    sin_lo = (sin - sin_hi.astype(np.float64)).astype(bf16)
    turn = 2.0 * np.pi / (A * B) * (np.outer(index, index) % (A * B))
    return cos_hi, sin_hi, cos_lo, sin_lo, np.cos(turn).astype(np.float32), np.sin(turn).astype(np.float32)


def matrices():
    cos_hi, sin_hi, cos_lo, sin_lo, turn_re, turn_im = (jnp.asarray(t) for t in tables())

    def real_form(re, im):
        return jnp.concatenate([jnp.concatenate([re, -im], axis=1), jnp.concatenate([im, re], axis=1)], axis=0)

    high, low = real_form(cos_hi, sin_hi), real_form(cos_lo, sin_lo)
    left = jnp.concatenate([high, low, high], axis=1)
    return left, left.T, turn_re, turn_im


def encode(scaled):
    cube = scaled * scaled * scaled
    sixth = cube * cube
    return sixth * sixth * cube


def decode(coded):
    size = jnp.exp2(jnp.log2(jnp.abs(coded)) * (1.0 / POWER))
    return jnp.where(coded < 0, -size, size)


def split(value):
    high = value.astype(jnp.bfloat16)
    return high, (value - high.astype(jnp.float32)).astype(jnp.bfloat16)


def left_dft(left, re, im):
    re_hi, re_lo = split(re)
    im_hi, im_lo = split(im)
    pieces = jnp.concatenate([re_hi, im_hi, re_hi, im_hi, re_lo, im_lo], axis=0)
    out = jnp.dot(left, pieces, preferred_element_type=jnp.float32)
    return out[:A], out[A:]


def right_dft(right, re, im):
    re_hi, re_lo = split(re)
    im_hi, im_lo = split(im)
    pieces = jnp.concatenate([re_hi, im_hi, re_hi, im_hi, re_lo, im_lo], axis=1)
    out = jnp.dot(pieces, right, preferred_element_type=jnp.float32)
    return out[:, :B], out[:, B:]


def short_conv(rows, before, taps, column):
    count = rows.shape[0]
    joined = jnp.concatenate([before, rows], axis=0)
    return (
        taps[0, column][None, :] * rows
        + taps[1, column][None, :] * joined[7 : 7 + count]
        + taps[2, column][None, :] * joined[6 : 6 + count]
    )


def pre_kernel(key_ref, value_ref, halo_ref, taps_ref, coded_ref, scale_ref, gated_ref):
    slabs = key_ref.shape[0] // B
    taps = taps_ref[...]

    def gate(slab, carry):
        key_before, value_before, most = carry
        rows = pl.ds(pl.multiple_of(slab * B, B), B)
        key = key_ref[rows, :].astype(jnp.float32)
        value = value_ref[rows, :].astype(jnp.float32)
        gated = short_conv(key, key_before, taps, 1) * short_conv(value, value_before, taps, 2)
        gated_ref[rows, :] = gated
        most = jnp.maximum(most, jnp.max(jnp.abs(gated).reshape(B // 8, 8, LANES), axis=0))
        return key[B - 8 :], value[B - 8 :], most

    start = (halo_ref[1].astype(jnp.float32), halo_ref[2].astype(jnp.float32), jnp.zeros((8, LANES), jnp.float32))
    _, _, most = lax.fori_loop(0, slabs, gate, start)
    most = jnp.maximum(jnp.max(most, axis=0, keepdims=True), LEAST)
    scale_ref[...] = most * (1.0 / TOP)
    factor = TOP / most

    def send(slab, _):
        rows = pl.ds(pl.multiple_of(slab * B, B), B)
        coded = encode(gated_ref[rows, :] * factor).T.astype(jnp.bfloat16)
        if len(coded_ref.shape) == 3:
            coded_ref[slab] = coded
        else:
            per = coded_ref.shape[2]
            for target in range(coded_ref.shape[0]):
                coded_ref[target, slab] = coded[target * per : (target + 1) * per]
        return 0

    lax.fori_loop(0, slabs, send, 0)


def spectrum_kernel(filter_ref, left_ref, right_ref, turn_re_ref, turn_im_ref, re_ref, im_ref):
    taps = filter_ref[...]
    re, im = left_dft(left_ref[...], taps, jnp.zeros_like(taps))
    cos, sin = turn_re_ref[...], turn_im_ref[...]
    re, im = right_dft(right_ref[...], re * cos + im * sin, im * cos - re * sin)
    re_ref[...] = re * (1.0 / (A * B))
    im_ref[...] = im * (1.0 / (A * B))


def conv_kernel(
    coded_ref, scale_ref, left_ref, right_ref, turn_re_ref, turn_im_ref, spec_re_ref, spec_im_ref,
    out_ref, out_scale_ref, work_ref,
):
    per = scale_ref.shape[1]

    def receive(slab, _):
        rows = pl.ds(pl.multiple_of(slab * A, A), A)
        value = decode(coded_ref[rows, :].astype(jnp.float32))
        for half in range(2):
            work_ref[half, rows, :] = value[:, half * LANES : (half + 1) * LANES]
        return 0

    lax.fori_loop(0, per, receive, 0)
    lane = lax.broadcasted_iota(jnp.int32, (A, per), 1)

    def signal(channel):
        scale = jnp.sum(jnp.where(lane == channel, scale_ref[...], 0.0), axis=1, keepdims=True)
        rows = pl.ds(channel, A, stride=per)
        return jnp.concatenate([work_ref[half, rows, :] for half in range(2)], axis=1) * scale

    def emit(channel, value):
        most = jnp.maximum(jnp.max(jnp.abs(value), keepdims=True), LEAST)
        out_scale_ref[pl.ds(channel, 1), :] = jnp.broadcast_to(most * (1.0 / TOP), (1, LANES))
        coded = encode(value * (TOP / most))
        for half in range(2):
            work_ref[half, pl.ds(channel, A, stride=per), :] = coded[:, half * LANES : (half + 1) * LANES]

    def pair(index, _):
        first, second = 2 * index, 2 * index + 1
        re, im = left_dft(left_ref[...], signal(first), signal(second))
        cos, sin = turn_re_ref[...], turn_im_ref[...]
        re, im = right_dft(right_ref[...], re * cos + im * sin, im * cos - re * sin)
        spec_re, spec_im = spec_re_ref[...], spec_im_ref[...]
        re, im = right_dft(right_ref[...], re * spec_re - im * spec_im, -(re * spec_im + im * spec_re))
        cos, sin = turn_re_ref[...], turn_im_ref[...]
        re, im = left_dft(left_ref[...], re * cos + im * sin, im * cos - re * sin)
        emit(first, re)
        emit(second, -im)
        return 0

    lax.fori_loop(0, per // 2, pair, 0)

    def send(slab, _):
        rows = pl.ds(pl.multiple_of(slab * A, A), A)
        out_ref[rows, :] = jnp.concatenate([work_ref[half, rows, :] for half in range(2)], axis=1).astype(jnp.bfloat16)
        return 0

    lax.fori_loop(0, per, send, 0)


def post_kernel(
    query_ref, key_ref, value_ref, halo_ref, taps_ref, skip_ref, coded_ref, scale_ref, *rest,
):
    out_ref, before_ref = rest[-2:]
    taps = taps_ref[...]
    slabs = query_ref.shape[0] // B

    @pl.when(pl.program_id(0) == 0)
    def _():
        before_ref[...] = halo_ref[...].astype(jnp.float32)

    def mix(slab, carry):
        query_before, key_before, value_before = carry
        rows = pl.ds(pl.multiple_of(slab * B, B), B)
        query = query_ref[rows, :].astype(jnp.float32)
        key = key_ref[rows, :].astype(jnp.float32)
        value = value_ref[rows, :].astype(jnp.float32)
        gated = short_conv(key, key_before, taps, 1) * short_conv(value, value_before, taps, 2)
        if len(coded_ref.shape) == 3:
            coded = coded_ref[slab]
        else:
            coded = jnp.concatenate([coded_ref[source, slab] for source in range(coded_ref.shape[0])], axis=0)
        convolved = decode(coded.astype(jnp.float32).T) * scale_ref[...]
        out_ref[rows, :] = short_conv(query, query_before, taps, 0) * (convolved + skip_ref[...] * gated)
        return query[B - 8 :], key[B - 8 :], value[B - 8 :]

    carry = lax.fori_loop(0, slabs, mix, (before_ref[0], before_ref[1], before_ref[2]))
    for which in range(3):
        before_ref[which] = carry[which]


def params():
    return pltpu.CompilerParams(vmem_limit_bytes=48 * 1024 * 1024)


def cost(flops, size):
    return pl.CostEstimate(flops=flops, bytes_accessed=size, transcendentals=0)


def per_device(query_proj, key_proj, value_proj, short_taps, skip_gain, long_filter):
    tok_count, chan_width = query_proj.shape
    seq_count = lax.axis_size("seq")
    slabs = tok_count // B
    chunks = chan_width // LANES
    per = LANES // seq_count
    aligned = per % 8 == 0

    ends = jnp.stack([query_proj[-8:], key_proj[-8:], value_proj[-8:]])
    halo = lax.ppermute(ends, "seq", [(source, source + 1) for source in range(seq_count - 1)])
    whole_filter = lax.all_gather(long_filter.reshape(slabs, B), "seq", axis=0, tiled=True)
    left, right, turn_re, turn_im = matrices()
    skip_row = skip_gain[None, :]

    coded_shape = (seq_count, slabs, per, B) if aligned else (slabs, LANES, B)
    swap = partial(lax.all_to_all, axis_name="seq", split_axis=0, concat_axis=0, tiled=True)

    def pre(chunk):
        coded, scale = pl.pallas_call(
            pre_kernel,
            grid=(1,),
            in_specs=[
                pl.BlockSpec((tok_count, LANES), lambda i: (0, chunk)),
                pl.BlockSpec((tok_count, LANES), lambda i: (0, chunk)),
                pl.BlockSpec((3, 8, LANES), lambda i: (0, 0, chunk)),
                pl.BlockSpec((3, 3, LANES), lambda i: (0, 0, chunk)),
            ],
            out_specs=[
                pl.BlockSpec(coded_shape, lambda i: (0,) * len(coded_shape)),
                pl.BlockSpec((1, LANES), lambda i: (0, 0)),
            ],
            out_shape=[
                jax.ShapeDtypeStruct(coded_shape, jnp.bfloat16),
                jax.ShapeDtypeStruct((1, LANES), jnp.float32),
            ],
            scratch_shapes=[pltpu.VMEM((tok_count, LANES), jnp.float32)],
            compiler_params=params(),
            cost_estimate=cost(40 * tok_count * LANES, 6 * tok_count * LANES),
            name="pre",
        )(key_proj, value_proj, halo, short_taps)
        if not aligned:
            coded = coded.reshape(slabs, seq_count, per, B).transpose(1, 0, 2, 3)
        return coded, scale.reshape(seq_count, per)

    def conv(coded, scale, spec_re, spec_im):
        rows = A * per
        return pl.pallas_call(
            conv_kernel,
            out_shape=[
                jax.ShapeDtypeStruct((rows, B), jnp.bfloat16),
                jax.ShapeDtypeStruct((per, LANES), jnp.float32),
            ],
            scratch_shapes=[pltpu.VMEM((2, rows, LANES), jnp.float32)],
            compiler_params=params(),
            cost_estimate=cost(per // 2 * 4 * 2 * 512 * 1536 * 256, 4 * rows * B),
            name="conv",
        )(coded.reshape(rows, B), jnp.repeat(scale, slabs, axis=0), left, right, turn_re, turn_im, spec_re, spec_im)

    def post(chunk, coded, scale, out):
        if not aligned:
            coded = coded.transpose(1, 0, 2, 3).reshape(slabs, LANES, B)
        step = min(1024, tok_count)
        block = step // B
        rows = pl.BlockSpec((step, LANES), lambda i: (i, chunk))
        coded_spec = (
            pl.BlockSpec((seq_count, block, per, B), lambda i: (0, i, 0, 0))
            if aligned
            else pl.BlockSpec((block, LANES, B), lambda i: (i, 0, 0))
        )
        in_specs = [
            rows,
            rows,
            rows,
            pl.BlockSpec((3, 8, LANES), lambda i: (0, 0, chunk)),
            pl.BlockSpec((3, 3, LANES), lambda i: (0, 0, chunk)),
            pl.BlockSpec((1, LANES), lambda i: (0, chunk)),
            coded_spec,
            pl.BlockSpec((1, LANES), lambda i: (0, 0)),
        ]
        args = [query_proj, key_proj, value_proj, halo, short_taps, skip_row, coded, scale]
        if out is not None:
            in_specs.append(pl.BlockSpec(memory_space=pl.ANY))
            args.append(out)
        return pl.pallas_call(
            post_kernel,
            grid=(tok_count // step,),
            in_specs=in_specs,
            out_specs=rows,
            out_shape=jax.ShapeDtypeStruct((tok_count, chan_width), jnp.float32),
            scratch_shapes=[pltpu.VMEM((3, 8, LANES), jnp.float32)],
            input_output_aliases={} if out is None else {len(args) - 1: 0},
            compiler_params=params(),
            cost_estimate=cost(60 * tok_count * LANES, 12 * tok_count * LANES),
            name="post",
        )(*args)

    spec_re, spec_im = pl.pallas_call(
        spectrum_kernel,
        out_shape=[jax.ShapeDtypeStruct((A, B), jnp.float32)] * 2,
        compiler_params=params(),
        cost_estimate=cost(2 * 2 * 512 * 1536 * 256, 4 * A * B),
        name="spectrum",
    )(whole_filter, left, right, turn_re, turn_im)

    received = []
    for chunk in range(chunks):
        coded, scale = pre(chunk)
        received.append((swap(coded), swap(scale)))
    returned = []
    for coded, scale in received:
        coded, scale = conv(coded, scale, spec_re, spec_im)
        coded = swap(coded.reshape(seq_count, slabs, per, B))
        scale = lax.all_gather(scale[:, 0], "seq", axis=0, tiled=True)
        returned.append((coded, scale.reshape(1, LANES)))
    out = None
    for chunk, (coded, scale) in enumerate(returned):
        out = post(chunk, coded, scale, out)
    return out


def solution(mesh):
    return jax.shard_map(
        per_device,
        mesh=mesh,
        in_specs=(
            P("seq", "chan"),
            P("seq", "chan"),
            P("seq", "chan"),
            P(None, None, "chan"),
            P("chan"),
            P("chan", "seq"),
        ),
        out_specs=P("seq", "chan"),
        check_vma=False,
    )
```

time: 2010 us -> 597 us (0.30)
  waiting for transfers between devices: 1060 us -> 31.1 us
  matrix products: 249 us -> 0 us
  Pallas kernels: 0 us -> 216 us
  local copies, waits for them, and re-layouts: 157 us -> 19.4 us
  other arithmetic: 126 us -> 3.23 us
  blocking collectives: 367 us -> 274 us
    all_to_all x5 -> x8, waiting for transfers between devices: 926 us -> 29.6 us  [the longest x4 29.6 us: per_device(): coded = swap(coded.reshape(seq_count, slabs, per, B))]
    dot_general x24 -> x0, matrix products: 249 us -> none  [the longest x6 70.2 us: complex_apply(): product(matrix_re, data_im) + product(matrix_im, data_re)]
    pallas_call x0 -> x13, Pallas kernels: none -> 216 us  [the longest x4 133 us: conv(): pl.pallas_call(conv_kernel, out_shape=[jax.ShapeDtypeStruct((rows, B), jn...]
    all_to_all x1 -> x4, blocking collectives: 367 us -> 161 us  [per_device(): received.append((swap(coded), swap(scale)))]
    ppermute x3 -> x1, waiting for transfers between devices: 130 us -> 1.5 us  [per_device(): lax.ppermute(ends, 'seq', [(source, source + 1) for source in range(seq_c...]
    mul x2 -> x0, other arithmetic: 73.2 us -> none  [the longest x1 39.5 us: per_device(): gated = key_short * value_short]
    all_gather x0 -> x1, blocking collectives: none -> 66.9 us  [per_device(): lax.all_gather(long_filter.reshape(slabs, B), 'seq', axis=0, tiled=True)]
    another operation x4 -> x2, local copies, waits for them, and re-layouts: 60.6 us -> 1.41 us  [per_device(): ends = jnp.stack([query_proj[-8:], key_proj[-8:], value_proj[-8:]])]
  transfers between devices with their start and end apart: 8 -> 9, of which waited for: 4 -> 4; matrix products, arithmetic and copies ran while one was open for 11% -> 1% of each run, Pallas kernels for 0% -> 33%
where the time goes in v1:
time: 597 us; the launch traced here: 590 us
  blocking collectives  274 us (46%)
  Pallas kernels  216 us (36%)
  starting transfers between devices  45 us (8%)
  waiting for transfers between devices  31.1 us (5%)
  local copies, waits for them, and re-layouts  19.4 us (3%)
    all_to_all x4, blocking collectives, per_device(): received.append((swap(coded), swap(scale)))  161 us
    pallas_call x4, Pallas kernels, conv(): pl.pallas_call(conv_kernel, out_shape=[jax.ShapeDtypeStruct((rows, B), jn...  133 us
    all_gather x1, blocking collectives, per_device(): lax.all_gather(long_filter.reshape(slabs, B), 'seq', axis=0, tiled=True)  66.9 us
    unnamed x1, blocking collectives  46.2 us
    pallas_call x4, Pallas kernels, post(): pl.pallas_call(post_kernel, grid=(tok_count // step,), in_specs=in_specs,...  44.1 us
    pallas_call x4, Pallas kernels, pre(): pl.pallas_call(pre_kernel, grid=(1,), in_specs=[pl.BlockSpec((tok_count,...  37.1 us
    all_to_all x4, waiting for transfers between devices, per_device(): coded = swap(coded.reshape(seq_count, slabs, per, B))  29.6 us
    all_to_all x4, starting transfers between devices, per_device(): received.append((swap(coded), swap(scale)))  23.1 us
  transfers between devices with their start and end apart: 9, of which 4 were waited for; matrix products, arithmetic and copies ran while one was open for 1% of the time, Pallas kernels for 33%

profile of v1, /device:TPU:0, one launch (start us, length us, event | category | flops | bytes accessed | tf_op | source)
XLA Modules:
  0.0 589.6 jit_solution(8796801317026572934)
XLA Ops:
  8.5 8.9 %pre.7 = (bf16[8,32,16,256]{3,2,1,0:T(8,128)(2,1)S(1)}, f32[1,128]{1,0:T(1,128)S(1)}) custom-call(bf16[8192,512]{1,0:T(8,128)(2,1)} %key_ref.15, bf16[8192,512]{1,0:T(8,128)(2,1)} %value_ref.15, bf16[3,8,512]{2,1,0:T(8,128)(2,1)S(1)} %collective-permute-done.halo_ref, f32[3,3,512]{2,1,0:T(4,128)S(1)} %copy-done.4), custom_call_target="tpu_custom_call" | custom-call | flops 41943040 | bytes 6291456 | tf_op jit(solution)/shard_map/pre/pallas_call | solution.py:236
  19.3 6.6 %all-to-all-start.10 = ((f32[8,1,16]{2,1,0:T(1,128)}), f32[8,1,16]{2,1,0:T(1,128)S(1)}, u32[]{:S(2)}, u32[]{:S(2)}) async-start(f32[8,1,16]{2,1,0:T(1,128)} %bitcast.24), calls=%async_computation.10 | async-start | bytes 8192 | tf_op jit(solution)/shard_map/all_to_all | solution.py:325
  25.9 8.9 %pre.6 = (bf16[8,32,16,256]{3,2,1,0:T(8,128)(2,1)S(1)}, f32[1,128]{1,0:T(1,128)S(1)}) custom-call(bf16[8192,512]{1,0:T(8,128)(2,1)} %key_ref.15, bf16[8192,512]{1,0:T(8,128)(2,1)} %value_ref.15, bf16[3,8,512]{2,1,0:T(8,128)(2,1)S(1)} %collective-permute-done.halo_ref, f32[3,3,512]{2,1,0:T(4,128)S(1)} %copy-done.5), custom_call_target="tpu_custom_call" | custom-call | flops 41943040 | bytes 6291456 | tf_op jit(solution)/shard_map/pre/pallas_call | solution.py:236
  37.5 6.0 %all-to-all-start.7 = ((f32[8,1,16]{2,1,0:T(1,128)}), f32[8,1,16]{2,1,0:T(1,128)S(1)}, u32[]{:S(2)}, u32[]{:S(2)}) async-start(f32[8,1,16]{2,1,0:T(1,128)} %bitcast.18), calls=%async_computation.7 | async-start | bytes 8192 | tf_op jit(solution)/shard_map/all_to_all | solution.py:325
  43.5 8.9 %pre.5 = (bf16[8,32,16,256]{3,2,1,0:T(8,128)(2,1)S(1)}, f32[1,128]{1,0:T(1,128)S(1)}) custom-call(bf16[8192,512]{1,0:T(8,128)(2,1)} %key_ref.15, bf16[8192,512]{1,0:T(8,128)(2,1)} %value_ref.15, bf16[3,8,512]{2,1,0:T(8,128)(2,1)S(1)} %collective-permute-done.halo_ref, f32[3,3,512]{2,1,0:T(4,128)S(1)} %copy-done.5), custom_call_target="tpu_custom_call" | custom-call | flops 41943040 | bytes 6291456 | tf_op jit(solution)/shard_map/pre/pallas_call | solution.py:236
  55.1 6.0 %all-to-all-start.4 = ((f32[8,1,16]{2,1,0:T(1,128)}), f32[8,1,16]{2,1,0:T(1,128)S(1)}, u32[]{:S(2)}, u32[]{:S(2)}) async-start(f32[8,1,16]{2,1,0:T(1,128)} %bitcast.12), calls=%async_computation.4 | async-start | bytes 8192 | tf_op jit(solution)/shard_map/all_to_all | solution.py:325
  61.1 10.3 %pre.4 = (bf16[8,32,16,256]{3,2,1,0:T(8,128)(2,1)}, f32[1,128]{1,0:T(1,128)S(1)}) custom-call(bf16[8192,512]{1,0:T(8,128)(2,1)} %key_ref.15, bf16[8192,512]{1,0:T(8,128)(2,1)} %value_ref.15, bf16[3,8,512]{2,1,0:T(8,128)(2,1)S(1)} %collective-permute-done.halo_ref, f32[3,3,512]{2,1,0:T(4,128)S(1)} %copy-done.5), custom_call_target="tpu_custom_call" | custom-call | flops 41943040 | bytes 6291456 | tf_op jit(solution)/shard_map/pre/pallas_call | solution.py:236
  72.1 12.3 %all_to_all.88 = f32[8,1,16]{2,1,0:T(1,128)S(1)} all-to-all(f32[8,1,16]{2,1,0:T(1,128)S(1)} %bitcast.55), channel_id=1, replica_groups=mesh['chan'=4,'seq'=8] {'seq'}, dimensions={0} | all-to-all | bytes 1024 | tf_op jit(solution)/shard_map/all_to_all | solution.py:325
  84.3 47.5 %all_to_all.89 = bf16[8,32,16,256]{3,2,1,0:T(8,128)(2,1)} all-to-all(bf16[8,32,16,256]{3,2,1,0:T(8,128)(2,1)S(1)} %get-tuple-element.37), channel_id=1, replica_groups=mesh['chan'=4,'seq'=8] {'seq'}, dimensions={0} | all-to-all | bytes 4194304 | tf_op jit(solution)/shard_map/all_to_all | solution.py:325
  131.9 50.2 %all_to_all.90 = bf16[8,32,16,256]{3,2,1,0:T(8,128)(2,1)} all-to-all(bf16[8,32,16,256]{3,2,1,0:T(8,128)(2,1)S(1)} %copy-done.1), channel_id=1, replica_groups=mesh['chan'=4,'seq'=8] {'seq'}, dimensions={0} | all-to-all | bytes 4194304 | tf_op jit(solution)/shard_map/all_to_all | solution.py:325
  182.1 50.7 %all_to_all.91 = bf16[8,32,16,256]{3,2,1,0:T(8,128)(2,1)} all-to-all(bf16[8,32,16,256]{3,2,1,0:T(8,128)(2,1)S(1)} %copy-done.3), channel_id=1, replica_groups=mesh['chan'=4,'seq'=8] {'seq'}, dimensions={0} | all-to-all | bytes 4194304 | tf_op jit(solution)/shard_map/all_to_all | solution.py:325
  238.0 66.9 %all_gather.15.filter_ref = f32[256,256]{1,0:T(8,128)S(1)} all-gather(f32[32,256]{1,0:T(8,128)S(1)} %reshape.69), channel_id=1, replica_groups=mesh['chan'=4,'seq'=8] {'seq'}, dimensions={0}, use_global_device_ids=true | all-gather | bytes 294912 | tf_op jit(solution)/shard_map/all_gather | solution.py:228
  308.2 33.3 %conv.7 = (bf16[4096,256]{1,0:T(8,128)(2,1)}, f32[16,128]{1,0:T(8,128)S(1)}) custom-call(bf16[4096,256]{1,0:T(8,128)(2,1)} %bitcast.47, f32[256,16]{1,0:T(8,128)S(1)} %bitcast.33, bf16[512,1536]{1,0:T(8,128)(2,1)S(1)} %copy-done.10, bf16[1536,512]{1,0:T(8,128)(2,1)S(1)} %copy-done.6, f32[256,256]{1,0:T(8,128)S(1)} %copy-done.15, f32[256,256]{1,0:T(8,128)S(1)} %copy-done.14, ...), custom_call_target="tpu_custom_call" | custom-call | flops 12884901888 | bytes 4194304 | tf_op jit(solution)/shard_map/conv/pallas_call | solution.py:264
  348.0 33.3 %conv.6 = (bf16[4096,256]{1,0:T(8,128)(2,1)}, f32[16,128]{1,0:T(8,128)S(1)}) custom-call(bf16[4096,256]{1,0:T(8,128)(2,1)} %bitcast.46, f32[256,16]{1,0:T(8,128)S(1)} %bitcast.34, bf16[512,1536]{1,0:T(8,128)(2,1)S(1)} %copy-done.11, bf16[1536,512]{1,0:T(8,128)(2,1)S(1)} %copy-done.7, f32[256,256]{1,0:T(8,128)S(1)} %copy-done.15, f32[256,256]{1,0:T(8,128)S(1)} %copy-done.14, ...), custom_call_target="tpu_custom_call" | custom-call | flops 12884901888 | bytes 4194304 | tf_op jit(solution)/shard_map/conv/pallas_call | solution.py:264
  381.3 7.3 %all-to-all-done.11.coded_ref = bf16[8,32,16,256]{3,2,1,0:T(8,128)(2,1)S(1)} async-done(((bf16[8,32,16,256]{3,2,1,0:T(8,128)(2,1)}), bf16[8,32,16,256]{3,2,1,0:T(8,128)(2,1)S(1)}, u32[]{:S(2)}, u32[]{:S(2)}) %all-to-all-start.11) | async-done | bytes 2097184 | tf_op jit(solution)/shard_map/all_to_all | solution.py:329
  395.8 33.2 %conv.5 = (bf16[4096,256]{1,0:T(8,128)(2,1)}, f32[16,128]{1,0:T(8,128)S(1)}) custom-call(bf16[4096,256]{1,0:T(8,128)(2,1)} %bitcast.45, f32[256,16]{1,0:T(8,128)S(1)} %bitcast.35, bf16[512,1536]{1,0:T(8,128)(2,1)S(1)} %copy-done.12, bf16[1536,512]{1,0:T(8,128)(2,1)S(1)} %copy-done.8, f32[256,256]{1,0:T(8,128)S(1)} %copy-done.15, f32[256,256]{1,0:T(8,128)S(1)} %copy-done.14, ...), custom_call_target="tpu_custom_call" | custom-call | flops 12884901888 | bytes 4194304 | tf_op jit(solution)/shard_map/conv/pallas_call | solution.py:264
  429.0 10.8 %all-to-all-done.8.coded_ref = bf16[8,32,16,256]{3,2,1,0:T(8,128)(2,1)} async-done(((bf16[8,32,16,256]{3,2,1,0:T(8,128)(2,1)}), bf16[8,32,16,256]{3,2,1,0:T(8,128)(2,1)}, u32[]{:S(2)}, u32[]{:S(2)}) %all-to-all-start.8) | async-done | bytes 2097184 | tf_op jit(solution)/shard_map/all_to_all | solution.py:329
  447.2 33.3 %conv.4 = (bf16[4096,256]{1,0:T(8,128)(2,1)}, f32[16,128]{1,0:T(8,128)S(1)}) custom-call(bf16[4096,256]{1,0:T(8,128)(2,1)} %bitcast.4.coded_ref, f32[256,16]{1,0:T(8,128)S(1)} %bitcast.32, bf16[512,1536]{1,0:T(8,128)(2,1)S(1)} %copy-done.13, bf16[1536,512]{1,0:T(8,128)(2,1)S(1)} %copy-done.9, f32[256,256]{1,0:T(8,128)S(1)} %copy-done.15, ...), custom_call_target="tpu_custom_call" | custom-call | flops 12884901888 | bytes 4194304 | tf_op jit(solution)/shard_map/conv/pallas_call | solution.py:264
  480.5 11.5 %all-to-all-done.5.coded_ref = bf16[8,32,16,256]{3,2,1,0:T(8,128)(2,1)} async-done(((bf16[8,32,16,256]{3,2,1,0:T(8,128)(2,1)}), bf16[8,32,16,256]{3,2,1,0:T(8,128)(2,1)}, u32[]{:S(2)}, u32[]{:S(2)}) %all-to-all-start.5) | async-done | bytes 2097184 | tf_op jit(solution)/shard_map/all_to_all | solution.py:329
  499.2 46.2 %all-reduce.4 = (f32[128]{0:T(128)S(1)}, f32[128]{0:T(128)S(1)}, f32[128]{0:T(128)S(1)}, f32[128]{0:T(128)S(1)}) all-reduce(f32[128]{0:T(128)S(1)} %dynamic-update-slice, f32[128]{0:T(128)S(1)} %dynamic-update-slice.1, f32[128]{0:T(128)S(1)} %dynamic-update-slice.2, f32[128]{0:T(128)S(1)} %dynamic-update-slice.3), channel_id=2, replica_groups=mesh['chan'=4,'seq'=8] {'seq'}, use_global_device_ids=true, to_apply=%add | all-reduce | flops 512 | bytes 4096
  545.4 10.7 %post.4.rest_0_ = f32[8192,512]{1,0:T(8,128)} custom-call(bf16[8192,512]{1,0:T(8,128)(2,1)} %query_ref.7, bf16[8192,512]{1,0:T(8,128)(2,1)} %key_ref.15, bf16[8192,512]{1,0:T(8,128)(2,1)} %value_ref.15, bf16[3,8,512]{2,1,0:T(8,128)(2,1)S(1)} %collective-permute-done.halo_ref, f32[3,3,512]{2,1,0:T(4,128)S(1)} %copy-done.5, f32[1,512]{1,0:T(1,128)S(1)} %bitcast.36, ...), custom_call_target="tpu_custom_call" | custom-call | flops 62914560 | bytes 12582912 | tf_op jit(solution)/shard_map/post/pallas_call | solution.py:301
  556.2 11.1 %post.5.rest_0_ = f32[8192,512]{1,0:T(8,128)} custom-call(bf16[8192,512]{1,0:T(8,128)(2,1)} %query_ref.7, bf16[8192,512]{1,0:T(8,128)(2,1)} %key_ref.15, bf16[8192,512]{1,0:T(8,128)(2,1)} %value_ref.15, bf16[3,8,512]{2,1,0:T(8,128)(2,1)S(1)} %collective-permute-done.halo_ref, f32[3,3,512]{2,1,0:T(4,128)S(1)} %copy-done.5, ...), custom_call_target="tpu_custom_call", output_to_operand_aliasing={{}: (8, {})} | custom-call | flops 62914560 | bytes 12582912 | tf_op jit(solution)/shard_map/post/pallas_call | solution.py:301
  567.3 11.1 %post.6.rest_0_ = f32[8192,512]{1,0:T(8,128)} custom-call(bf16[8192,512]{1,0:T(8,128)(2,1)} %query_ref.7, bf16[8192,512]{1,0:T(8,128)(2,1)} %key_ref.15, bf16[8192,512]{1,0:T(8,128)(2,1)} %value_ref.15, bf16[3,8,512]{2,1,0:T(8,128)(2,1)S(1)} %collective-permute-done.halo_ref, f32[3,3,512]{2,1,0:T(4,128)S(1)} %copy-done.5, ...), custom_call_target="tpu_custom_call", output_to_operand_aliasing={{}: (8, {})} | custom-call | flops 62914560 | bytes 12582912 | tf_op jit(solution)/shard_map/post/pallas_call | solution.py:301
  578.4 11.1 %post.7 = f32[8192,512]{1,0:T(8,128)} custom-call(bf16[8192,512]{1,0:T(8,128)(2,1)} %query_ref.7, bf16[8192,512]{1,0:T(8,128)(2,1)} %key_ref.15, bf16[8192,512]{1,0:T(8,128)(2,1)} %value_ref.15, bf16[3,8,512]{2,1,0:T(8,128)(2,1)S(1)} %collective-permute-done.halo_ref, f32[3,3,512]{2,1,0:T(4,128)S(1)} %copy-done.5, ...), custom_call_target="tpu_custom_call", output_to_operand_aliasing={{}: (8, {})} | custom-call | flops 62914560 | bytes 12582912 | tf_op jit(solution)/shard_map/post/pallas_call | solution.py:301
  (82 shorter events, 52.3 us)
Async XLA Ops:
  1.4 24.5 %copy-start.5 = (f32[3,3,512]{2,1,0:T(4,128)S(1)}, f32[3,3,512]{2,1,0:T(4,128)}, u32[]{:S(2)}) copy-start(f32[3,3,512]{2,1,0:T(4,128)} %taps_ref.15) | copy-start | bytes 55300
  1.4 6.4 %collective-permute-start = (bf16[3,8,512]{2,1,0:T(8,128)(2,1)S(1)}, bf16[3,8,512]{2,1,0:T(8,128)(2,1)S(1)}, u32[]{:S(2)}, u32[]{:S(2)}) collective-permute-start(bf16[3,8,512]{2,1,0:T(8,128)(2,1)S(1)} %pad_maximum_fusion), channel_id=1, source_target_pairs={{0,1},{1,2},{2,3},{3,4},{4,5},{5,6},{6,7},{8,9},{9,10},{10,11},{11... | collective-permute-start | bytes 73736 | tf_op jit(solution)/shard_map/ppermute | solution.py:227
  19.3 18.2 %all-to-all-start.10 = ((f32[8,1,16]{2,1,0:T(1,128)}), f32[8,1,16]{2,1,0:T(1,128)S(1)}, u32[]{:S(2)}, u32[]{:S(2)}) async-start(f32[8,1,16]{2,1,0:T(1,128)} %bitcast.24), calls=%async_computation.10 | async-start | bytes 8192 | tf_op jit(solution)/shard_map/all_to_all | solution.py:325
  37.5 17.6 %all-to-all-start.7 = ((f32[8,1,16]{2,1,0:T(1,128)}), f32[8,1,16]{2,1,0:T(1,128)S(1)}, u32[]{:S(2)}, u32[]{:S(2)}) async-start(f32[8,1,16]{2,1,0:T(1,128)} %bitcast.18), calls=%async_computation.7 | async-start | bytes 8192 | tf_op jit(solution)/shard_map/all_to_all | solution.py:325
  55.1 17.0 %all-to-all-start.4 = ((f32[8,1,16]{2,1,0:T(1,128)}), f32[8,1,16]{2,1,0:T(1,128)S(1)}, u32[]{:S(2)}, u32[]{:S(2)}) async-start(f32[8,1,16]{2,1,0:T(1,128)} %bitcast.12), calls=%async_computation.4 | async-start | bytes 8192 | tf_op jit(solution)/shard_map/all_to_all | solution.py:325
  84.3 47.5 %copy-start.1 = (bf16[8,32,16,256]{3,2,1,0:T(8,128)(2,1)S(1)}, bf16[8,32,16,256]{3,2,1,0:T(8,128)(2,1)}, u32[]{:S(2)}) copy-start(bf16[8,32,16,256]{3,2,1,0:T(8,128)(2,1)} %copy-done) | copy-start | bytes 6291460
  131.9 50.2 %copy-start.3 = (bf16[8,32,16,256]{3,2,1,0:T(8,128)(2,1)S(1)}, bf16[8,32,16,256]{3,2,1,0:T(8,128)(2,1)}, u32[]{:S(2)}) copy-start(bf16[8,32,16,256]{3,2,1,0:T(8,128)(2,1)} %copy-done.2) | copy-start | bytes 6291460
  232.8 4.5 copy-start.17
  232.8 72.1 %copy-start.6 = (bf16[1536,512]{1,0:T(8,128)(2,1)S(1)}, bf16[1536,512]{1,0:T(8,128)(2,1)}, u32[]{:S(2)}) copy-start(bf16[1536,512]{1,0:T(8,128)(2,1)} %constant.28.right_ref) | copy-start | bytes 4718596
  232.8 72.1 %copy-start.14 = (f32[256,256]{1,0:T(8,128)S(1)}, f32[256,256]{1,0:T(8,128)}, u32[]{:S(2)}) copy-start(f32[256,256]{1,0:T(8,128)} %constant.17.clone.turn_im_ref) | copy-start | bytes 786436
  232.8 72.1 %copy-start.15 = (f32[256,256]{1,0:T(8,128)S(1)}, f32[256,256]{1,0:T(8,128)}, u32[]{:S(2)}) copy-start(f32[256,256]{1,0:T(8,128)} %constant.16.clone.turn_re_ref) | copy-start | bytes 786436
  232.8 108.7 %all-to-all-start = ((bf16[8,32,16,256]{3,2,1,0:T(8,128)(2,1)}), bf16[8,32,16,256]{3,2,1,0:T(8,128)(2,1)}, u32[]{:S(2)}, u32[]{:S(2)}) async-start(bf16[8,32,16,256]{3,2,1,0:T(8,128)(2,1)} %get-tuple-element.23), calls=%async_computation | async-start | bytes 4194304 | tf_op jit(solution)/shard_map/all_to_all | solution.py:325
  304.9 1.4 copy-start.10
  341.5 47.1 %all-to-all-start.11 = ((bf16[8,32,16,256]{3,2,1,0:T(8,128)(2,1)}), bf16[8,32,16,256]{3,2,1,0:T(8,128)(2,1)S(1)}, u32[]{:S(2)}, u32[]{:S(2)}) async-start(bf16[8,32,16,256]{3,2,1,0:T(8,128)(2,1)} %bitcast.49), calls=%async_computation.11 | async-start | bytes 4194304 | tf_op jit(solution)/shard_map/all_to_all | solution.py:329
  345.2 1.4 copy-start.7
  388.6 51.2 %all-to-all-start.8 = ((bf16[8,32,16,256]{3,2,1,0:T(8,128)(2,1)}), bf16[8,32,16,256]{3,2,1,0:T(8,128)(2,1)}, u32[]{:S(2)}, u32[]{:S(2)}) async-start(bf16[8,32,16,256]{3,2,1,0:T(8,128)(2,1)} %bitcast.50), calls=%async_computation.8 | async-start | bytes 4194304 | tf_op jit(solution)/shard_map/all_to_all | solution.py:329
  393.0 1.4 copy-start.8
  394.4 1.4 copy-start.12
  439.8 52.2 %all-to-all-start.5 = ((bf16[8,32,16,256]{3,2,1,0:T(8,128)(2,1)}), bf16[8,32,16,256]{3,2,1,0:T(8,128)(2,1)}, u32[]{:S(2)}, u32[]{:S(2)}) async-start(bf16[8,32,16,256]{3,2,1,0:T(8,128)(2,1)} %bitcast.48), calls=%async_computation.5 | async-start | bytes 4194304 | tf_op jit(solution)/shard_map/all_to_all | solution.py:329
  444.4 1.4 copy-start.9
  445.8 1.4 copy-start.13
  492.0 4.5 copy-start.18
  492.0 53.4 %copy-start.16 = (f32[512]{0:T(512)S(1)}, f32[512]{0:T(512)}, u32[]{:S(2)}) copy-start(f32[512]{0:T(512)} %param.16) | copy-start | bytes 6148
  492.0 86.4 %all-to-all-start.2 = ((bf16[8,32,16,256]{3,2,1,0:T(8,128)(2,1)}), bf16[8,32,16,256]{3,2,1,0:T(8,128)(2,1)}, u32[]{:S(2)}, u32[]{:S(2)}) async-start(bf16[8,32,16,256]{3,2,1,0:T(8,128)(2,1)} %bitcast.44), calls=%async_computation.2 | async-start | bytes 4194304 | tf_op jit(solution)/shard_map/all_to_all | solution.py:329
  (4 other events, 4.8 us)

commit v2 on v1

v2 whole, which is shorter than its diff:
```python
from functools import partial

import jax
import jax.numpy as jnp
import numpy as np
from jax import lax
from jax.experimental import pallas as pl
from jax.experimental.pallas import tpu as pltpu
from jax.sharding import PartitionSpec as P

A = 256
B = 256
LANES = 128
EXTRA = 8

POWER = 15
TOP = 2.0**8.375
LEAST = 1e-34


def tables():
    index = np.arange(A)
    angle = 2.0 * np.pi / A * (np.outer(index, index) % A)
    cos, sin = np.cos(angle), -np.sin(angle)
    bf16 = jnp.bfloat16
    cos_hi, sin_hi = cos.astype(bf16), sin.astype(bf16)
    cos_lo = (cos - cos_hi.astype(np.float64)).astype(bf16)
    sin_lo = (sin - sin_hi.astype(np.float64)).astype(bf16)
    turn = 2.0 * np.pi / (A * B) * (np.outer(index, index) % (A * B))
    return cos_hi, sin_hi, cos_lo, sin_lo, np.cos(turn).astype(np.float32), np.sin(turn).astype(np.float32)


def encode(scaled):
    cube = scaled * scaled * scaled
    sixth = cube * cube
    return sixth * sixth * cube


def decode(coded):
    size = jnp.exp2(jnp.log2(jnp.abs(coded)) * (1.0 / POWER))
    return jnp.where(coded < 0, -size, size)


def split(value):
    high = value.astype(jnp.bfloat16)
    return high, (value - high.astype(jnp.float32)).astype(jnp.bfloat16)


def left_dft(left, pairs):
    high, low = split(jnp.concatenate([part for pair in pairs for part in pair], axis=1))
    out = jnp.dot(left, jnp.concatenate([high, high, low], axis=0), preferred_element_type=jnp.float32)
    result = []
    for index in range(len(pairs)):
        re, im = (out[:, (2 * index + part) * B : (2 * index + part + 1) * B] for part in range(2))
        result.append((re[:A] - im[A:], im[:A] + re[A:]))
    return result


def right_dft(right, pairs):
    pieces = []
    for re, im in pairs:
        re_hi, re_lo = split(re)
        im_hi, im_lo = split(im)
        pieces.append(jnp.concatenate([re_hi, im_hi, re_hi, im_hi, re_lo, im_lo], axis=1))
    out = jnp.dot(jnp.concatenate(pieces, axis=0), right, preferred_element_type=jnp.float32)
    return [(out[index * A : (index + 1) * A, :B], out[index * A : (index + 1) * A, B:]) for index in range(len(pairs))]


def turn(pairs, turn_re_ref, turn_im_ref):
    cos, sin = turn_re_ref[...], turn_im_ref[...]
    return [(re * cos + im * sin, im * cos - re * sin) for re, im in pairs]


def short_conv(rows, before, taps, column):
    count = rows.shape[0]
    joined = jnp.concatenate([before, rows], axis=0)
    return (
        taps[0, column][None, :] * rows
        + taps[1, column][None, :] * joined[7 : 7 + count]
        + taps[2, column][None, :] * joined[6 : 6 + count]
    )


def gate_all(key_ref, value_ref, halo_ref, taps_ref, gated_ref):
    taps = taps_ref[...]

    def gate(slab, carry):
        key_before, value_before, most = carry
        rows = pl.ds(pl.multiple_of(slab * B, B), B)
        key = key_ref[rows, :].astype(jnp.float32)
        value = value_ref[rows, :].astype(jnp.float32)
        gated = short_conv(key, key_before, taps, 1) * short_conv(value, value_before, taps, 2)
        gated_ref[rows, :] = gated
        most = jnp.maximum(most, jnp.max(jnp.abs(gated).reshape(B // 8, 8, LANES), axis=0))
        return key[B - 8 :], value[B - 8 :], most

    start = (halo_ref[1].astype(jnp.float32), halo_ref[2].astype(jnp.float32), jnp.zeros((8, LANES), jnp.float32))
    _, _, most = lax.fori_loop(0, key_ref.shape[0] // B, gate, start)
    return scale_of(jnp.max(most, axis=0, keepdims=True))


def scale_of(most):
    return (jnp.maximum(most, LEAST) * (1.0 / TOP)).astype(jnp.bfloat16).astype(jnp.float32)


def scale_tile(scale):
    return jnp.broadcast_to(jnp.concatenate([scale, scale], axis=1), (EXTRA, B)).astype(jnp.bfloat16)


def pre_whole_kernel(key_ref, value_ref, halo_ref, taps_ref, coded_ref, scale_ref, gated_ref):
    scale = gate_all(key_ref, value_ref, halo_ref, taps_ref, gated_ref)
    scale_ref[...] = scale
    factor = 1.0 / scale

    def send(slab, _):
        rows = pl.ds(pl.multiple_of(slab * B, B), B)
        coded_ref[slab] = encode(gated_ref[rows, :] * factor).T.astype(jnp.bfloat16)
        return 0

    lax.fori_loop(0, coded_ref.shape[0], send, 0)


def pre_parts_kernel(per, key_ref, value_ref, halo_ref, taps_ref, *rest):
    filter_refs, (parts_ref, gated_ref) = rest[:-2], rest[-2:]
    count, _, size, _ = parts_ref.shape
    slabs = key_ref.shape[0] // B
    scale = gate_all(key_ref, value_ref, halo_ref, taps_ref, gated_ref)
    factor = 1.0 / scale

    def send(slab, _):
        rows = pl.ds(pl.multiple_of(slab * B, B), B)
        coded = encode(gated_ref[rows, :] * factor).T.astype(jnp.bfloat16)
        place = pl.ds(pl.multiple_of(slab * per, per), per)
        for target in range(count):
            parts_ref[target, 0, place, :] = coded[target * per : (target + 1) * per]
        return 0

    lax.fori_loop(0, slabs, send, 0)
    tile = scale_tile(scale)
    for target in range(count):
        for filter_ref in filter_refs:
            parts_ref[target, 0, slabs * per : size - EXTRA, :] = jnp.concatenate(split(filter_ref[...]), axis=0)
        parts_ref[target, 0, size - EXTRA :, :] = tile


def parts_spectrum_kernel(parts_ref, *refs):
    *refs, filter_ref = refs
    slabs = parts_ref.shape[2] // 2
    for source in range(parts_ref.shape[0]):
        both = parts_ref[source, 0].astype(jnp.float32)
        filter_ref[source * slabs : (source + 1) * slabs, :] = both[:slabs] + both[slabs:]
    spectrum_kernel(filter_ref, *refs)


def spectrum_kernel(filter_ref, *refs):
    cos_hi, sin_hi, cos_lo, sin_lo = (ref[...] for ref in refs[:4])
    turn_re_ref, turn_im_ref, re_ref, im_ref, left_ref, right_ref = refs[4:]
    for piece, (cos, sin) in enumerate(((cos_hi, sin_hi), (cos_lo, sin_lo), (cos_hi, sin_hi))):
        left_ref[:A, piece * A : (piece + 1) * A] = cos
        left_ref[A:, piece * A : (piece + 1) * A] = sin
        right_ref[2 * piece * B : (2 * piece + 1) * B, :B] = cos
        right_ref[2 * piece * B : (2 * piece + 1) * B, B:] = sin
        right_ref[(2 * piece + 1) * B : (2 * piece + 2) * B, :B] = -sin
        right_ref[(2 * piece + 1) * B : (2 * piece + 2) * B, B:] = cos
    taps = filter_ref[...]
    pairs = left_dft(left_ref[...], [(taps, jnp.zeros_like(taps))])
    ((re, im),) = right_dft(right_ref[...], turn(pairs, turn_re_ref, turn_im_ref))
    re_ref[...] = re * (1.0 / (A * B))
    im_ref[...] = im * (1.0 / (A * B))


def put(work_ref, rows, value):
    for part in range(2):
        work_ref[part, rows, :] = value[:, part * LANES : (part + 1) * LANES]


def take(work_ref, rows):
    return jnp.concatenate([work_ref[part, rows, :] for part in range(2)], axis=1)


def convolve_all(per, base, scale_ref, left_ref, right_ref, turn_re_ref, turn_im_ref, spec_re_ref, spec_im_ref, work_ref):
    lane = lax.broadcasted_iota(jnp.int32, (A, LANES), 1)
    row_lane = lax.broadcasted_iota(jnp.int32, (1, LANES), 1)

    def signal(channel):
        scale = jnp.sum(jnp.where(lane == base + channel, scale_ref[...], 0.0), axis=1, keepdims=True)
        return take(work_ref, pl.ds(channel, A, stride=per)) * scale

    def emit(channel, value, scales):
        scale = scale_of(jnp.max(jnp.abs(value), keepdims=True))
        put(work_ref, pl.ds(channel, A, stride=per), encode(value * (1.0 / scale)))
        return jnp.where(row_lane == base + channel, scale, scales)

    together = 2 if per % 4 == 0 else 1

    def convolve(index, scales):
        first = 2 * together * index
        pairs = [(signal(first + 2 * which), signal(first + 2 * which + 1)) for which in range(together)]
        pairs = turn(left_dft(left_ref[...], pairs), turn_re_ref, turn_im_ref)
        pairs = right_dft(right_ref[...], pairs)
        spec_re, spec_im = spec_re_ref[...], spec_im_ref[...]
        pairs = [(re * spec_re - im * spec_im, -(re * spec_im + im * spec_re)) for re, im in pairs]
        pairs = turn(right_dft(right_ref[...], pairs), turn_re_ref, turn_im_ref)
        pairs = left_dft(left_ref[...], pairs)
        for which, (re, im) in enumerate(pairs):
            scales = emit(first + 2 * which, re, scales)
            scales = emit(first + 2 * which + 1, -im, scales)
        return scales

    return lax.fori_loop(0, per // (2 * together), convolve, jnp.zeros((1, LANES), jnp.float32))


def conv_whole_kernel(coded_ref, scale_ref, *rest):
    constants, (out_ref, out_scale_ref, work_ref) = rest[:6], rest[6:]
    per = coded_ref.shape[0] // A

    def receive(slab, _):
        rows = pl.ds(pl.multiple_of(slab * A, A), A)
        put(work_ref, rows, decode(coded_ref[rows, :].astype(jnp.float32)))
        return 0

    lax.fori_loop(0, per, receive, 0)
    scales = convolve_all(per, 0, scale_ref, *constants, work_ref)
    out_scale_ref[...] = jnp.broadcast_to(scales, out_scale_ref.shape)

    def send(slab, _):
        rows = pl.ds(pl.multiple_of(slab * A, A), A)
        out_ref[rows, :] = take(work_ref, rows).astype(jnp.bfloat16)
        return 0

    lax.fori_loop(0, per, send, 0)


def conv_parts_kernel(per, place_ref, parts_ref, *rest):
    constants, (out_ref, work_ref, scale_ref) = rest[:6], rest[6:]
    count, _, size, _ = parts_ref.shape
    out_size = out_ref.shape[2]
    slabs = A // count
    block = slabs * per
    steps = block // A

    def receive(index, _):
        for step in range(steps):
            value = parts_ref[index, 0, step * A : (step + 1) * A, :].astype(jnp.float32)
            put(work_ref, pl.ds(pl.multiple_of(index * block + step * A, A), A), decode(value))
        row = parts_ref[index, 0, size - EXTRA :, :LANES].astype(jnp.float32)[:1]
        scale_ref[pl.ds(pl.multiple_of(index * slabs, slabs), slabs), :] = jnp.broadcast_to(row, (slabs, LANES))
        return 0

    lax.fori_loop(0, count, receive, 0)
    tile = scale_tile(convolve_all(per, place_ref[0] * per, scale_ref, *constants, work_ref))

    def send(index, _):
        for step in range(steps):
            value = take(work_ref, pl.ds(pl.multiple_of(index * block + step * A, A), A))
            out_ref[index, 0, step * A : (step + 1) * A, :] = value.astype(jnp.bfloat16)
        out_ref[index, 0, out_size - EXTRA :, :] = tile
        return 0

    lax.fori_loop(0, count, send, 0)


def mix_all(step, query_ref, key_ref, value_ref, halo_ref, taps_ref, skip_ref, convolved_of, out_ref, before_ref):
    taps = taps_ref[...]

    @pl.when(step == 0)
    def _():
        before_ref[...] = halo_ref[...].astype(jnp.float32)

    def mix(slab, carry):
        query_before, key_before, value_before = carry
        rows = pl.ds(pl.multiple_of(slab * B, B), B)
        query = query_ref[rows, :].astype(jnp.float32)
        key = key_ref[rows, :].astype(jnp.float32)
        value = value_ref[rows, :].astype(jnp.float32)
        gated = short_conv(key, key_before, taps, 1) * short_conv(value, value_before, taps, 2)
        out_ref[rows, :] = short_conv(query, query_before, taps, 0) * (convolved_of(slab) + skip_ref[...] * gated)
        return query[B - 8 :], key[B - 8 :], value[B - 8 :]

    carry = lax.fori_loop(0, query_ref.shape[0] // B, mix, (before_ref[0], before_ref[1], before_ref[2]))
    for which in range(3):
        before_ref[which] = carry[which]


def post_whole_kernel(*refs):
    inputs, (coded_ref, scale_ref), (out_ref, before_ref) = refs[:6], refs[6:8], refs[-2:]

    def convolved_of(slab):
        return decode(coded_ref[slab].astype(jnp.float32).T) * scale_ref[...]

    mix_all(pl.program_id(0), *inputs, convolved_of, out_ref, before_ref)


def post_parts_kernel(*refs):
    inputs, (parts_ref, ends_ref), (out_ref, before_ref) = refs[:6], refs[6:8], refs[-2:]
    count = parts_ref.shape[0]
    per = LANES // count
    scale = jnp.zeros((EXTRA, LANES), jnp.float32)
    for source in range(count):
        scale = scale + ends_ref[source, 0].astype(jnp.float32)[:, :LANES]
    scale = scale[:1]

    def convolved_of(slab):
        place = pl.ds(pl.multiple_of(slab * per, per), per)
        coded = jnp.concatenate([parts_ref[source, 0, place, :] for source in range(count)], axis=0)
        return decode(coded.astype(jnp.float32).T) * scale

    mix_all(pl.program_id(1), *inputs, convolved_of, out_ref, before_ref)


def params():
    return pltpu.CompilerParams(vmem_limit_bytes=48 * 1024 * 1024)


def cost(flops, size):
    return pl.CostEstimate(flops=flops // 1000, bytes_accessed=size // 1000, transcendentals=0)


SCALAR = pl.BlockSpec(memory_space=pltpu.SMEM)


def per_device(query_proj, key_proj, value_proj, short_taps, skip_gain, long_filter):
    tok_count, chan_width = query_proj.shape
    seq_count = lax.axis_size("seq")
    slabs = tok_count // B
    chunks = chan_width // LANES
    per = LANES // seq_count
    in_parts = per % 16 == 0 and (slabs * per) % A == 0 and slabs % 8 == 0 and seq_count & (seq_count - 1) == 0
    size = slabs * per + EXTRA
    place = lax.axis_index("seq").astype(jnp.int32).reshape(1)

    ends = jnp.stack([query_proj[-8:], key_proj[-8:], value_proj[-8:]])
    halo = lax.ppermute(ends, "seq", [(source, source + 1) for source in range(seq_count - 1)])
    skip_row = skip_gain[None, :]

    swap = partial(lax.all_to_all, axis_name="seq", split_axis=0, concat_axis=0, tiled=True)

    def whole_block(shape):
        return pl.BlockSpec(shape, lambda i: (0,) * len(shape))

    def pre(chunk, count, *filters):
        rows = pl.BlockSpec((tok_count, LANES), lambda i: (0, chunk + i))
        if in_parts:
            rows_out = size + 2 * slabs * len(filters)
            out_shape = [jax.ShapeDtypeStruct((seq_count, count, rows_out, B), jnp.bfloat16)]
            out_specs = [pl.BlockSpec((seq_count, 1, rows_out, B), lambda i: (0, i, 0, 0))]
        else:
            out_shape = [
                jax.ShapeDtypeStruct((slabs, LANES, B), jnp.bfloat16),
                jax.ShapeDtypeStruct((1, LANES), jnp.float32),
            ]
            out_specs = [whole_block(out.shape) for out in out_shape]
        return pl.pallas_call(
            partial(pre_parts_kernel, per) if in_parts else pre_whole_kernel,
            grid=(count,),
            in_specs=[
                rows,
                rows,
                pl.BlockSpec((3, 8, LANES), lambda i: (0, 0, chunk + i)),
                pl.BlockSpec((3, 3, LANES), lambda i: (0, 0, chunk + i)),
            ]
            + [whole_block((slabs, B))] * len(filters),
            out_specs=out_specs,
            out_shape=out_shape,
            scratch_shapes=[pltpu.VMEM((tok_count, LANES), jnp.float32)],
            compiler_params=params(),
            cost_estimate=cost(count * 40 * tok_count * LANES, count * 6 * tok_count * LANES),
            name="pre",
        )(key_proj, value_proj, halo, short_taps, *filters)

    def conv(first, count, coded, *scale):
        rows = A * per
        args = (coded, *scale, left, right, turn_re, turn_im, spec_re, spec_im)
        in_specs = [whole_block(arg.shape) for arg in args]
        scratch = [pltpu.VMEM((2, rows, LANES), jnp.float32)]
        if in_parts:
            args = (place,) + args
            block = (seq_count, 1, coded.shape[2], B)
            in_specs = [SCALAR, pl.BlockSpec(block, lambda i: (0, first + i, 0, 0))] + in_specs[1:]
            out_shape = [jax.ShapeDtypeStruct((seq_count, count, size, B), jnp.bfloat16)]
            out_specs = [pl.BlockSpec((seq_count, 1, size, B), lambda i: (0, i, 0, 0))]
            scratch.append(pltpu.VMEM((A, LANES), jnp.float32))
        else:
            out_shape = [
                jax.ShapeDtypeStruct((rows, B), jnp.bfloat16),
                jax.ShapeDtypeStruct((8, LANES), jnp.float32),
            ]
            out_specs = [whole_block(out.shape) for out in out_shape]
        return pl.pallas_call(
            partial(conv_parts_kernel, per) if in_parts else conv_whole_kernel,
            grid=(count,),
            in_specs=in_specs,
            out_specs=out_specs,
            out_shape=out_shape,
            scratch_shapes=scratch,
            compiler_params=params(),
            cost_estimate=cost(count * per // 2 * 4 * 2 * 512 * 1536 * 256, count * 4 * rows * B),
            name="conv",
        )(*args)

    def post(chunk, count, out, coded, *scale):
        step = min(1024, tok_count)
        block = step // B
        rows = pl.BlockSpec((step, LANES), lambda u, i: (i, chunk + u))
        in_specs = [
            rows,
            rows,
            rows,
            pl.BlockSpec((3, 8, LANES), lambda u, i: (0, 0, chunk + u)),
            pl.BlockSpec((3, 3, LANES), lambda u, i: (0, 0, chunk + u)),
            pl.BlockSpec((1, LANES), lambda u, i: (0, chunk + u)),
        ]
        args = [query_proj, key_proj, value_proj, halo, short_taps, skip_row]
        if in_parts:
            last = slabs * per // EXTRA
            in_specs += [
                pl.BlockSpec((seq_count, 1, block * per, B), lambda u, i: (0, u, i, 0)),
                pl.BlockSpec((seq_count, 1, EXTRA, B), lambda u, i: (0, u, last, 0)),
            ]
            args += [coded, coded]
        else:
            in_specs += [
                pl.BlockSpec((block, LANES, B), lambda u, i: (i, 0, 0)),
                pl.BlockSpec((1, LANES), lambda u, i: (0, 0)),
            ]
            args += [coded, *scale]
        if out is not None:
            in_specs.append(pl.BlockSpec(memory_space=pl.ANY))
            args.append(out)
        return pl.pallas_call(
            post_parts_kernel if in_parts else post_whole_kernel,
            grid=(count, tok_count // step),
            in_specs=in_specs,
            out_specs=rows,
            out_shape=jax.ShapeDtypeStruct((tok_count, chan_width), jnp.float32),
            scratch_shapes=[pltpu.VMEM((3, 8, LANES), jnp.float32)],
            input_output_aliases={} if out is None else {len(args) - 1: 0},
            compiler_params=params(),
            cost_estimate=cost(count * 60 * tok_count * LANES, count * 12 * tok_count * LANES),
            name="post",
        )(*args)

    own_filter = long_filter.reshape(slabs, B)
    if in_parts:
        arrived = [(0, swap(*pre(0, 1, own_filter)))]
        if chunks > 1:
            arrived.append((1, swap(*pre(1, chunks - 1))))
        whole_filter = arrived[0][1]
        filter_spec = pl.BlockSpec((seq_count, 1, 2 * slabs, B), lambda i: (0, 0, per // 2, 0))
    else:
        whole_filter = swap(jnp.broadcast_to(own_filter, (seq_count, slabs, B))).reshape(A, B)
        filter_spec = whole_block((A, B))
    cos_hi, sin_hi, cos_lo, sin_lo, turn_re, turn_im = (jnp.asarray(table) for table in tables())
    filter_args = (whole_filter, cos_hi, sin_hi, cos_lo, sin_lo, turn_re, turn_im)
    spec_shape = [jax.ShapeDtypeStruct((A, B), jnp.float32)] * 2
    spec_shape += [jax.ShapeDtypeStruct((2 * A, 3 * A), jnp.bfloat16), jax.ShapeDtypeStruct((6 * B, 2 * B), jnp.bfloat16)]
    spec_re, spec_im, left, right = pl.pallas_call(
        parts_spectrum_kernel if in_parts else spectrum_kernel,
        grid=(1,),
        in_specs=[filter_spec] + [whole_block((A, B))] * 6,
        out_specs=[whole_block(out.shape) for out in spec_shape],
        out_shape=spec_shape,
        scratch_shapes=[pltpu.VMEM((A, B), jnp.float32)] * in_parts,
        compiler_params=params(),
        cost_estimate=cost(2 * 2 * 512 * 1536 * 256, 16 * A * B),
        name="spectrum",
    )(*filter_args)

    out = None
    if in_parts:
        cuts = sorted({0, 1, chunks - 1, chunks})
        returned = []
        for start, stop in zip(cuts[:-1], cuts[1:]):
            source, coded = arrived[min(start, 1)]
            returned.append((start, stop - start, swap(*conv(start - source, stop - start, coded))))
        for start, count, coded in returned:
            out = post(start, count, out, coded)
    else:
        returned = []
        for chunk in range(chunks):
            coded, scale = pre(chunk, 1)
            coded = swap(coded.reshape(slabs, seq_count, per, B).transpose(1, 0, 2, 3))
            scale = jnp.repeat(swap(scale.reshape(seq_count, per)), slabs, axis=0)
            scale = jnp.pad(scale, ((0, 0), (0, LANES - per)))
            coded, scale = conv(0, 1, coded.reshape(A * per, B), scale)
            coded = swap(coded.reshape(seq_count, slabs, per, B))
            scale = lax.all_gather(scale[0, :per], "seq", axis=0, tiled=True)
            returned.append((coded.transpose(1, 0, 2, 3).reshape(slabs, LANES, B), scale.reshape(1, LANES)))
        for chunk, (coded, scale) in enumerate(returned):
            out = post(chunk, 1, out, coded, scale)
    return out


def solution(mesh):
    return jax.shard_map(
        per_device,
        mesh=mesh,
        in_specs=(
            P("seq", "chan"),
            P("seq", "chan"),
            P("seq", "chan"),
            P(None, None, "chan"),
            P("chan"),
            P("chan", "seq"),
        ),
        out_specs=P("seq", "chan"),
        check_vma=False,
    )
```

time: 597 us -> 442 us (0.74); the launches traced: 590 us -> 441 us
  blocking collectives: 274 us -> 0 us
  waiting for transfers between devices: 31.1 us -> 222 us
  Pallas kernels: 216 us -> 172 us
  starting transfers between devices: 45 us -> 29.7 us
    all_to_all x8 -> x5, waiting for transfers between devices: 29.6 us -> 222 us  [the longest x1 109 us: per_device(): arrived.append((1, swap(*pre(1, chunks - 1))))]
    all_to_all x4 -> x0, blocking collectives: 161 us -> none  [per_device(): received.append((swap(coded), swap(scale)))]
    all_gather x1 -> x0, blocking collectives: 66.9 us -> none  [per_device(): lax.all_gather(long_filter.reshape(slabs, B), 'seq', axis=0, tiled=True)]
    unnamed x1 -> x0, blocking collectives: 46.2 us -> none
    pallas_call x13 -> x9, Pallas kernels: 216 us -> 172 us  [the longest x3 92.6 us: conv(): pl.pallas_call(partial(conv_parts_kernel, per) if in_parts else conv_whol...]
    all_to_all x8 -> x5, starting transfers between devices: 40.2 us -> 24.9 us  [the longest x3 14 us: per_device(): swap(*conv(start - source, stop - start, coded))]
    unnamed x47 -> x41, local copies, waits for them, and re-layouts: 14.8 us -> 13.2 us
  transfers between devices with their start and end apart: 9 -> 6, of which waited for: 4 -> 4; matrix products, arithmetic and copies ran while one was open for 1% -> 0% of each run, Pallas kernels for 33% -> 34%
where the time goes in v2:
time: 442 us; the launch traced here: 441 us
  waiting for transfers between devices  222 us (50%)
  Pallas kernels  172 us (39%)
  starting transfers between devices  29.7 us (7%)
  local copies, waits for them, and re-layouts  14.6 us (3%)
    all_to_all x1, waiting for transfers between devices, per_device(): arrived.append((1, swap(*pre(1, chunks - 1))))  109 us
    pallas_call x3, Pallas kernels, conv(): pl.pallas_call(partial(conv_parts_kernel, per) if in_parts else conv_whol...  92.6 us
    all_to_all x3, waiting for transfers between devices, per_device(): swap(*conv(start - source, stop - start, coded))  83.3 us
    pallas_call x3, Pallas kernels, post(): pl.pallas_call(post_parts_kernel if in_parts else post_whole_kernel, grid...  42.7 us
    pallas_call x2, Pallas kernels, pre(): pl.pallas_call(partial(pre_parts_kernel, per) if in_parts else pre_whole_...  34.2 us
    all_to_all x1, waiting for transfers between devices, per_device(): arrived = [(0, swap(*pre(0, 1, own_filter)))]  29.7 us
    all_to_all x3, starting transfers between devices, per_device(): swap(*conv(start - source, stop - start, coded))  14 us
    unnamed x41, local copies, waits for them, and re-layouts  13.2 us
  transfers between devices with their start and end apart: 6, of which 4 were waited for; matrix products, arithmetic and copies ran while one was open for 0% of the time, Pallas kernels for 34%

profile of v2, /device:TPU:0, one launch (start us, length us, event | category | flops | bytes accessed | tf_op | source)
XLA Modules:
  0.0 440.5 jit_solution(4000977082045021861)
XLA Ops:
  1.4 4.8 %collective-permute-start = (bf16[3,8,512]{2,1,0:T(8,128)(2,1)S(1)}, bf16[3,8,512]{2,1,0:T(8,128)(2,1)S(1)}, u32[]{:S(2)}, u32[]{:S(2)}) collective-permute-start(bf16[3,8,512]{2,1,0:T(8,128)(2,1)S(1)} %pad_maximum_fusion), channel_id=1, source_target_pairs={{0,1},{1,2},{2,3},{3,4},{4,5},{5,6},{6,7},{8,9},{9,10},{10,11},{11... | collective-permute-start | bytes 73736 | tf_op jit(solution)/shard_map/ppermute | solution.py:333
  6.8 1.5 reduce.3
  9.0 10.4 %pre.3 = bf16[8,1,584,256]{3,2,1,0:T(8,128)(2,1)} custom-call(bf16[8192,512]{1,0:T(8,128)(2,1)} %refs_1_.6, bf16[8192,512]{1,0:T(8,128)(2,1)} %refs_2_.6, bf16[3,8,512]{2,1,0:T(8,128)(2,1)S(1)} %collective-permute-done.halo_ref.refs_3_, f32[3,3,512]{2,1,0:T(4,128)S(1)} %copy-done.13, f32[32,256]{1,0:T(8,128)S(1)} %reshape.7.rest_0_), custom_call_target="tpu_custom_call" | custom-call | flops 41943 | bytes 6291 | tf_op jit(solution)/shard_map/pre/pallas_call | solution.py:353
  19.4 6.1 %all-to-all-start.1 = ((bf16[8,1,584,256]{3,2,1,0:T(8,128)(2,1)}), bf16[8,1,584,256]{3,2,1,0:T(8,128)(2,1)}, u32[]{:S(2)}, u32[]{:S(2)}) async-start(bf16[8,1,584,256]{3,2,1,0:T(8,128)(2,1)} %pre.3), calls=%async_computation.1 | async-start | bytes 4784128 | tf_op jit(solution)/shard_map/all_to_all | solution.py:445
  25.5 23.8 %pre.2 = bf16[8,3,520,256]{3,2,1,0:T(8,128)(2,1)} custom-call(bf16[8192,512]{1,0:T(8,128)(2,1)} %refs_1_.6, bf16[8192,512]{1,0:T(8,128)(2,1)} %refs_2_.6, bf16[3,8,512]{2,1,0:T(8,128)(2,1)S(1)} %collective-permute-done.halo_ref.refs_3_, f32[3,3,512]{2,1,0:T(4,128)S(1)} %copy-done.14), custom_call_target="tpu_custom_call" | custom-call | flops 125829 | bytes 18874 | tf_op jit(solution)/shard_map/pre/pallas_call | solution.py:353
  49.4 29.7 %all-to-all-done.1.parts_ref = bf16[8,1,584,256]{3,2,1,0:T(8,128)(2,1)} async-done(((bf16[8,1,584,256]{3,2,1,0:T(8,128)(2,1)}), bf16[8,1,584,256]{3,2,1,0:T(8,128)(2,1)}, u32[]{:S(2)}, u32[]{:S(2)}) %all-to-all-start.1) | async-done | bytes 2392096 | tf_op jit(solution)/shard_map/all_to_all | solution.py:445
  79.0 4.8 %all-to-all-start = ((bf16[8,3,520,256]{3,2,1,0:T(8,128)(2,1)}), bf16[8,3,520,256]{3,2,1,0:T(8,128)(2,1)}, u32[]{:S(2)}, u32[]{:S(2)}) async-start(bf16[8,3,520,256]{3,2,1,0:T(8,128)(2,1)} %pre.2), calls=%async_computation | async-start | bytes 12779520 | tf_op jit(solution)/shard_map/all_to_all | solution.py:447
  83.9 2.9 spectrum.1
  86.8 23.3 %conv.5 = bf16[8,1,520,256]{3,2,1,0:T(8,128)(2,1)S(1)} custom-call(s32[1]{0:T(128)} %bitcast.4.place_ref, bf16[8,1,584,256]{3,2,1,0:T(8,128)(2,1)} %all-to-all-done.1.parts_ref, bf16[512,768]{1,0:T(8,128)(2,1)S(1)} %get-tuple-element.9.rest_0_, bf16[1536,512]{1,0:T(8,128)(2,1)S(1)} %get-tuple-element.10.rest_1_, f32[256,256]{1,0:T(8,128)S(1)} %copy-done.6, ...), custom_call_target="tpu_custom_call" | custom-call | flops 12884901 | bytes 4194 | tf_op jit(solution)/shard_map/conv/pallas_call | solution.py:389
  111.2 1.4 copy-done.4
  114.0 109.2 %all-to-all-done.parts_ref = bf16[8,3,520,256]{3,2,1,0:T(8,128)(2,1)} async-done(((bf16[8,3,520,256]{3,2,1,0:T(8,128)(2,1)}), bf16[8,3,520,256]{3,2,1,0:T(8,128)(2,1)}, u32[]{:S(2)}, u32[]{:S(2)}) %all-to-all-start) | async-done | bytes 6389792 | tf_op jit(solution)/shard_map/all_to_all | solution.py:447
  223.2 3.6 all-to-all-start.4
  226.8 1.4 copy-done.1
  230.1 46.1 %conv.4 = bf16[8,2,520,256]{3,2,1,0:T(8,128)(2,1)} custom-call(s32[1]{0:T(128)} %bitcast.4.place_ref, bf16[8,3,520,256]{3,2,1,0:T(8,128)(2,1)} %all-to-all-done.parts_ref, bf16[512,768]{1,0:T(8,128)(2,1)S(1)} %get-tuple-element.9.rest_0_, bf16[1536,512]{1,0:T(8,128)(2,1)S(1)} %copy-done.1, f32[256,256]{1,0:T(8,128)S(1)} %copy-done.6, ...), custom_call_target="tpu_custom_call" | custom-call | flops 25769804 | bytes 8388 | tf_op jit(solution)/shard_map/conv/pallas_call | solution.py:389
  276.3 6.0 %all-to-all-start.3 = ((bf16[8,2,520,256]{3,2,1,0:T(8,128)(2,1)}), bf16[8,2,520,256]{3,2,1,0:T(8,128)(2,1)}, u32[]{:S(2)}, u32[]{:S(2)}) async-start(bf16[8,2,520,256]{3,2,1,0:T(8,128)(2,1)} %conv.4), calls=%async_computation.3 | async-start | bytes 8519680 | tf_op jit(solution)/shard_map/all_to_all | solution.py:475
  282.3 1.4 copy-done.2
  285.6 23.2 %conv.3 = bf16[8,1,520,256]{3,2,1,0:T(8,128)(2,1)S(1)} custom-call(s32[1]{0:T(128)} %bitcast.4.place_ref, bf16[8,3,520,256]{3,2,1,0:T(8,128)(2,1)} %all-to-all-done.parts_ref, bf16[512,768]{1,0:T(8,128)(2,1)S(1)} %get-tuple-element.9.rest_0_, bf16[1536,512]{1,0:T(8,128)(2,1)S(1)} %copy-done.2, f32[256,256]{1,0:T(8,128)S(1)} %copy-done.6, ...), custom_call_target="tpu_custom_call" | custom-call | flops 12884901 | bytes 4194 | tf_op jit(solution)/shard_map/conv/pallas_call | solution.py:389
  308.8 1.3 copy-done.3
  310.1 66.4 %all-to-all-done.3.refs_6_.refs_7_ = bf16[8,2,520,256]{3,2,1,0:T(8,128)(2,1)} async-done(((bf16[8,2,520,256]{3,2,1,0:T(8,128)(2,1)}), bf16[8,2,520,256]{3,2,1,0:T(8,128)(2,1)}, u32[]{:S(2)}, u32[]{:S(2)}) %all-to-all-start.3) | async-done | bytes 4259872 | tf_op jit(solution)/shard_map/all_to_all | solution.py:475
  376.5 4.4 all-to-all-start.2
  380.9 10.8 %post.3.refs_8_ = f32[8192,512]{1,0:T(8,128)} custom-call(bf16[8192,512]{1,0:T(8,128)(2,1)} %refs_0_.6, bf16[8192,512]{1,0:T(8,128)(2,1)} %refs_1_.6, bf16[8192,512]{1,0:T(8,128)(2,1)} %refs_2_.6, bf16[3,8,512]{2,1,0:T(8,128)(2,1)S(1)} %collective-permute-done.halo_ref.refs_3_, f32[3,3,512]{2,1,0:T(4,128)S(1)} %copy-done.14, f32[1,512]{1,0:T(1,128)S(1)} %bitcast.8, ...), custom_call_target="tpu_custom_call" | custom-call | flops 62914 | bytes 12582 | tf_op jit(solution)/shard_map/post/pallas_call | solution.py:430
  391.7 20.8 %post.4.refs_8_ = f32[8192,512]{1,0:T(8,128)} custom-call(bf16[8192,512]{1,0:T(8,128)(2,1)} %refs_0_.6, bf16[8192,512]{1,0:T(8,128)(2,1)} %refs_1_.6, bf16[8192,512]{1,0:T(8,128)(2,1)} %refs_2_.6, bf16[3,8,512]{2,1,0:T(8,128)(2,1)S(1)} %collective-permute-done.halo_ref.refs_3_, f32[3,3,512]{2,1,0:T(4,128)S(1)} %copy-done.14, ...), custom_call_target="tpu_custom_call", output_to_operand_aliasing={{}: (8, {})} | custom-call | flops 125829 | bytes 25165 | tf_op jit(solution)/shard_map/post/pallas_call | solution.py:430
  412.4 16.9 %all-to-all-done.2.refs_6_.refs_7_ = bf16[8,1,520,256]{3,2,1,0:T(8,128)(2,1)} async-done(((bf16[8,1,520,256]{3,2,1,0:T(8,128)(2,1)}), bf16[8,1,520,256]{3,2,1,0:T(8,128)(2,1)}, u32[]{:S(2)}, u32[]{:S(2)}) %all-to-all-start.2) | async-done | bytes 2129952 | tf_op jit(solution)/shard_map/all_to_all | solution.py:475
  429.4 11.2 %post.5 = f32[8192,512]{1,0:T(8,128)} custom-call(bf16[8192,512]{1,0:T(8,128)(2,1)} %refs_0_.6, bf16[8192,512]{1,0:T(8,128)(2,1)} %refs_1_.6, bf16[8192,512]{1,0:T(8,128)(2,1)} %refs_2_.6, bf16[3,8,512]{2,1,0:T(8,128)(2,1)S(1)} %collective-permute-done.halo_ref.refs_3_, f32[3,3,512]{2,1,0:T(4,128)S(1)} %copy-done.14, ...), custom_call_target="tpu_custom_call", output_to_operand_aliasing={{}: (8, {})} | custom-call | flops 62914 | bytes 12582 | tf_op jit(solution)/shard_map/post/pallas_call | solution.py:430
  (43 shorter events, 9.1 us)
Async XLA Ops:
  1.4 6.9 %collective-permute-start = (bf16[3,8,512]{2,1,0:T(8,128)(2,1)S(1)}, bf16[3,8,512]{2,1,0:T(8,128)(2,1)S(1)}, u32[]{:S(2)}, u32[]{:S(2)}) collective-permute-start(bf16[3,8,512]{2,1,0:T(8,128)(2,1)S(1)} %pad_maximum_fusion), channel_id=1, source_target_pairs={{0,1},{1,2},{2,3},{3,4},{4,5},{5,6},{6,7},{8,9},{9,10},{10,11},{11... | collective-permute-start | bytes 73736 | tf_op jit(solution)/shard_map/ppermute | solution.py:333
  8.3 0.7 copy-start.13
  9.0 16.5 %copy-start.14 = (f32[3,3,512]{2,1,0:T(4,128)S(1)}, f32[3,3,512]{2,1,0:T(4,128)}, u32[]{:S(2)}) copy-start(f32[3,3,512]{2,1,0:T(4,128)} %refs_4_.6) | copy-start | bytes 55300
  19.4 59.6 %all-to-all-start.1 = ((bf16[8,1,584,256]{3,2,1,0:T(8,128)(2,1)}), bf16[8,1,584,256]{3,2,1,0:T(8,128)(2,1)}, u32[]{:S(2)}, u32[]{:S(2)}) async-start(bf16[8,1,584,256]{3,2,1,0:T(8,128)(2,1)} %pre.3), calls=%async_computation.1 | async-start | bytes 4784128 | tf_op jit(solution)/shard_map/all_to_all | solution.py:445
  49.3 34.5 %copy-start.5 = (f32[256,256]{1,0:T(8,128)S(1)}, f32[256,256]{1,0:T(8,128)}, u32[]{:S(2)}) copy-start(f32[256,256]{1,0:T(8,128)} %constant.21.clone.refs_5_.rest_3_) | copy-start | bytes 786436
  49.3 34.5 %copy-start.6 = (f32[256,256]{1,0:T(8,128)S(1)}, f32[256,256]{1,0:T(8,128)}, u32[]{:S(2)}) copy-start(f32[256,256]{1,0:T(8,128)} %constant.20.clone.refs_4_.rest_2_) | copy-start | bytes 786436
  49.3 34.5 %copy-start.15 = (bf16[256,256]{1,0:T(8,128)(2,1)S(1)}, bf16[256,256]{1,0:T(8,128)(2,1)}, u32[]{:S(2)}) copy-start(bf16[256,256]{1,0:T(8,128)(2,1)} %constant.19.clone.refs_3_) | copy-start | bytes 393220
  49.3 34.5 %copy-start.16 = (bf16[256,256]{1,0:T(8,128)(2,1)S(1)}, bf16[256,256]{1,0:T(8,128)(2,1)}, u32[]{:S(2)}) copy-start(bf16[256,256]{1,0:T(8,128)(2,1)} %constant.18.clone.refs_2_) | copy-start | bytes 393220
  49.3 34.5 %copy-start.17 = (bf16[256,256]{1,0:T(8,128)(2,1)S(1)}, bf16[256,256]{1,0:T(8,128)(2,1)}, u32[]{:S(2)}) copy-start(bf16[256,256]{1,0:T(8,128)(2,1)} %constant.17.clone.refs_1_) | copy-start | bytes 393220
  49.3 34.5 %copy-start.18 = (bf16[256,256]{1,0:T(8,128)(2,1)S(1)}, bf16[256,256]{1,0:T(8,128)(2,1)}, u32[]{:S(2)}) copy-start(bf16[256,256]{1,0:T(8,128)(2,1)} %constant.16.clone.refs_0_) | copy-start | bytes 393220
  79.0 144.2 %all-to-all-start = ((bf16[8,3,520,256]{3,2,1,0:T(8,128)(2,1)}), bf16[8,3,520,256]{3,2,1,0:T(8,128)(2,1)}, u32[]{:S(2)}, u32[]{:S(2)}) async-start(bf16[8,3,520,256]{3,2,1,0:T(8,128)(2,1)} %pre.2), calls=%async_computation | async-start | bytes 12779520 | tf_op jit(solution)/shard_map/all_to_all | solution.py:447
  110.0 1.2 copy-start
  111.2 1.4 copy-start.4
  223.2 53.1 %all-to-all-start.4 = ((bf16[8,1,520,256]{3,2,1,0:T(8,128)(2,1)}), bf16[8,1,520,256]{3,2,1,0:T(8,128)(2,1)S(1)}, u32[]{:S(2)}, u32[]{:S(2)}) async-start(bf16[8,1,520,256]{3,2,1,0:T(8,128)(2,1)} %copy-done.4), calls=%async_computation.4 | async-start | bytes 4259840 | tf_op jit(solution)/shard_map/all_to_all | solution.py:475
  226.8 1.4 copy-start.1
  228.2 0.9 copy-start.8
  229.2 0.9 copy-start.11
  276.3 100.2 %all-to-all-start.3 = ((bf16[8,2,520,256]{3,2,1,0:T(8,128)(2,1)}), bf16[8,2,520,256]{3,2,1,0:T(8,128)(2,1)}, u32[]{:S(2)}, u32[]{:S(2)}) async-start(bf16[8,2,520,256]{3,2,1,0:T(8,128)(2,1)} %conv.4), calls=%async_computation.3 | async-start | bytes 8519680 | tf_op jit(solution)/shard_map/all_to_all | solution.py:475
  282.3 1.4 copy-start.2
  283.7 0.9 copy-start.9
  284.6 0.9 copy-start.12
  285.6 95.3 %copy-start.19 = (f32[512]{0:T(512)S(1)}, f32[512]{0:T(512)}, u32[]{:S(2)}) copy-start(f32[512]{0:T(512)} %param.16) | copy-start | bytes 6148
  308.8 1.3 copy-start.3
  376.5 52.9 %all-to-all-start.2 = ((bf16[8,1,520,256]{3,2,1,0:T(8,128)(2,1)}), bf16[8,1,520,256]{3,2,1,0:T(8,128)(2,1)}, u32[]{:S(2)}, u32[]{:S(2)}) async-start(bf16[8,1,520,256]{3,2,1,0:T(8,128)(2,1)} %copy-done.3), calls=%async_computation.2 | async-start | bytes 4259840 | tf_op jit(solution)/shard_map/all_to_all | solution.py:475
  (2 other events, 1.4 us)

commit v3 on v2

--- a/solution.py
+++ b/solution.py
@@ -71,31 +71,30 @@
     return [(re * cos + im * sin, im * cos - re * sin) for re, im in pairs]
 
 
-def short_conv(rows, before, taps, column):
-    count = rows.shape[0]
-    joined = jnp.concatenate([before, rows], axis=0)
+def short_conv(window_ref, which, rows, taps, column):
+    window_ref[which, :8, :] = window_ref[which, B:, :]
+    window_ref[which, 8:, :] = rows
     return (
         taps[0, column][None, :] * rows
-        + taps[1, column][None, :] * joined[7 : 7 + count]
-        + taps[2, column][None, :] * joined[6 : 6 + count]
+        + taps[1, column][None, :] * window_ref[which, 7 : 7 + B, :]
+        + taps[2, column][None, :] * window_ref[which, 6 : 6 + B, :]
     )
 
 
-def gate_all(key_ref, value_ref, halo_ref, taps_ref, gated_ref):
+def gate_all(key_ref, value_ref, halo_ref, taps_ref, gated_ref, window_ref):
     taps = taps_ref[...]
-
-    def gate(slab, carry):
-        key_before, value_before, most = carry
+    for which in range(1, 3):
+        window_ref[which, B:, :] = halo_ref[which].astype(jnp.float32)
+
+    def gate(slab, most):
         rows = pl.ds(pl.multiple_of(slab * B, B), B)
-        key = key_ref[rows, :].astype(jnp.float32)
-        value = value_ref[rows, :].astype(jnp.float32)
-        gated = short_conv(key, key_before, taps, 1) * short_conv(value, value_before, taps, 2)
+        key = short_conv(window_ref, 1, key_ref[rows, :].astype(jnp.float32), taps, 1)
+        value = short_conv(window_ref, 2, value_ref[rows, :].astype(jnp.float32), taps, 2)
+        gated = key * value
         gated_ref[rows, :] = gated
-        most = jnp.maximum(most, jnp.max(jnp.abs(gated).reshape(B // 8, 8, LANES), axis=0))
-        return key[B - 8 :], value[B - 8 :], most
-
-    start = (halo_ref[1].astype(jnp.float32), halo_ref[2].astype(jnp.float32), jnp.zeros((8, LANES), jnp.float32))
-    _, _, most = lax.fori_loop(0, key_ref.shape[0] // B, gate, start)
+        return jnp.maximum(most, jnp.max(jnp.abs(gated).reshape(B // 8, 8, LANES), axis=0))
+
+    most = lax.fori_loop(0, key_ref.shape[0] // B, gate, jnp.zeros((8, LANES), jnp.float32))
     return scale_of(jnp.max(most, axis=0, keepdims=True))
 
 
@@ -107,29 +106,29 @@
     return jnp.broadcast_to(jnp.concatenate([scale, scale], axis=1), (EXTRA, B)).astype(jnp.bfloat16)
 
 
-def pre_whole_kernel(key_ref, value_ref, halo_ref, taps_ref, coded_ref, scale_ref, gated_ref):
-    scale = gate_all(key_ref, value_ref, halo_ref, taps_ref, gated_ref)
+def pre_whole_kernel(key_ref, value_ref, halo_ref, taps_ref, coded_ref, scale_ref, gated_ref, window_ref):
+    scale = gate_all(key_ref, value_ref, halo_ref, taps_ref, gated_ref, window_ref)
     scale_ref[...] = scale
     factor = 1.0 / scale
 
     def send(slab, _):
         rows = pl.ds(pl.multiple_of(slab * B, B), B)
-        coded_ref[slab] = encode(gated_ref[rows, :] * factor).T.astype(jnp.bfloat16)
+        coded_ref[slab] = encode(gated_ref[rows, :] * factor).astype(jnp.bfloat16).T
         return 0
 
     lax.fori_loop(0, coded_ref.shape[0], send, 0)
 
 
 def pre_parts_kernel(per, key_ref, value_ref, halo_ref, taps_ref, *rest):
-    filter_refs, (parts_ref, gated_ref) = rest[:-2], rest[-2:]
+    filter_refs, (parts_ref, gated_ref, window_ref) = rest[:-3], rest[-3:]
     count, _, size, _ = parts_ref.shape
     slabs = key_ref.shape[0] // B
-    scale = gate_all(key_ref, value_ref, halo_ref, taps_ref, gated_ref)
+    scale = gate_all(key_ref, value_ref, halo_ref, taps_ref, gated_ref, window_ref)
     factor = 1.0 / scale
 
     def send(slab, _):
         rows = pl.ds(pl.multiple_of(slab * B, B), B)
-        coded = encode(gated_ref[rows, :] * factor).T.astype(jnp.bfloat16)
+        coded = encode(gated_ref[rows, :] * factor).astype(jnp.bfloat16).T
         place = pl.ds(pl.multiple_of(slab * per, per), per)
         for target in range(count):
             parts_ref[target, 0, place, :] = coded[target * per : (target + 1) * per]
@@ -232,7 +231,14 @@
 
 
 def conv_parts_kernel(per, place_ref, parts_ref, *rest):
-    constants, (out_ref, work_ref, scale_ref) = rest[:6], rest[6:]
+    sources, (out_ref, work_ref, scale_ref), constants, sems = rest[:6], rest[6:9], rest[9:15], rest[15]
+    copies = [pltpu.make_async_copy(*pair, sems.at[index]) for index, pair in enumerate(zip(sources, constants))]
+
+    @pl.when(pl.program_id(0) == 0)
+    def _():
+        for copy in copies:
+            copy.start()
+
     count, _, size, _ = parts_ref.shape
     out_size = out_ref.shape[2]
     slabs = A // count
@@ -248,6 +254,12 @@
         return 0
 
     lax.fori_loop(0, count, receive, 0)
+
+    @pl.when(pl.program_id(0) == 0)
+    def _():
+        for copy in copies:
+            copy.wait()
+
     tile = scale_tile(convolve_all(per, place_ref[0] * per, scale_ref, *constants, work_ref))
 
     def send(index, _):
@@ -260,39 +272,37 @@
     lax.fori_loop(0, count, send, 0)
 
 
-def mix_all(step, query_ref, key_ref, value_ref, halo_ref, taps_ref, skip_ref, convolved_of, out_ref, before_ref):
+def mix_all(step, query_ref, key_ref, value_ref, halo_ref, taps_ref, skip_ref, convolved_of, out_ref, window_ref):
     taps = taps_ref[...]
 
     @pl.when(step == 0)
     def _():
-        before_ref[...] = halo_ref[...].astype(jnp.float32)
-
-    def mix(slab, carry):
-        query_before, key_before, value_before = carry
+        for which in range(3):
+            window_ref[which, B:, :] = halo_ref[which].astype(jnp.float32)
+
+    def mix(slab, _):
         rows = pl.ds(pl.multiple_of(slab * B, B), B)
-        query = query_ref[rows, :].astype(jnp.float32)
-        key = key_ref[rows, :].astype(jnp.float32)
-        value = value_ref[rows, :].astype(jnp.float32)
-        gated = short_conv(key, key_before, taps, 1) * short_conv(value, value_before, taps, 2)
-        out_ref[rows, :] = short_conv(query, query_before, taps, 0) * (convolved_of(slab) + skip_ref[...] * gated)
-        return query[B - 8 :], key[B - 8 :], value[B - 8 :]
-
-    carry = lax.fori_loop(0, query_ref.shape[0] // B, mix, (before_ref[0], before_ref[1], before_ref[2]))
-    for which in range(3):
-        before_ref[which] = carry[which]
+        query, key, value = (
+            short_conv(window_ref, which, ref[rows, :].astype(jnp.float32), taps, which)
+            for which, ref in enumerate((query_ref, key_ref, value_ref))
+        )
+        out_ref[rows, :] = query * (convolved_of(slab) + skip_ref[...] * (key * value))
+        return 0
+
+    lax.fori_loop(0, query_ref.shape[0] // B, mix, 0)
 
 
 def post_whole_kernel(*refs):
-    inputs, (coded_ref, scale_ref), (out_ref, before_ref) = refs[:6], refs[6:8], refs[-2:]
+    inputs, (coded_ref, scale_ref), (out_ref, window_ref) = refs[:6], refs[6:8], refs[-2:]
 
     def convolved_of(slab):
-        return decode(coded_ref[slab].astype(jnp.float32).T) * scale_ref[...]
-
-    mix_all(pl.program_id(0), *inputs, convolved_of, out_ref, before_ref)
+        return decode(coded_ref[slab].T.astype(jnp.float32)) * scale_ref[...]
+
+    mix_all(pl.program_id(0), *inputs, convolved_of, out_ref, window_ref)
 
 
 def post_parts_kernel(*refs):
-    inputs, (parts_ref, ends_ref), (out_ref, before_ref) = refs[:6], refs[6:8], refs[-2:]
+    inputs, (parts_ref, ends_ref), (out_ref, window_ref) = refs[:6], refs[6:8], refs[-2:]
     count = parts_ref.shape[0]
     per = LANES // count
     scale = jnp.zeros((EXTRA, LANES), jnp.float32)
@@ -303,9 +313,9 @@
     def convolved_of(slab):
         place = pl.ds(pl.multiple_of(slab * per, per), per)
         coded = jnp.concatenate([parts_ref[source, 0, place, :] for source in range(count)], axis=0)
-        return decode(coded.astype(jnp.float32).T) * scale
-
-    mix_all(pl.program_id(1), *inputs, convolved_of, out_ref, before_ref)
+        return decode(coded.T.astype(jnp.float32)) * scale
+
+    mix_all(pl.program_id(1), *inputs, convolved_of, out_ref, window_ref)
 
 
 def params():
@@ -362,7 +372,7 @@
             + [whole_block((slabs, B))] * len(filters),
             out_specs=out_specs,
             out_shape=out_shape,
-            scratch_shapes=[pltpu.VMEM((tok_count, LANES), jnp.float32)],
+            scratch_shapes=[pltpu.VMEM((tok_count, LANES), jnp.float32), pltpu.VMEM((3, 8 + B, LANES), jnp.float32)],
             compiler_params=params(),
             cost_estimate=cost(count * 40 * tok_count * LANES, count * 6 * tok_count * LANES),
             name="pre",
@@ -376,10 +386,12 @@
         if in_parts:
             args = (place,) + args
             block = (seq_count, 1, coded.shape[2], B)
-            in_specs = [SCALAR, pl.BlockSpec(block, lambda i: (0, first + i, 0, 0))] + in_specs[1:]
+            in_specs = [SCALAR, pl.BlockSpec(block, lambda i: (0, first + i, 0, 0))]
+            in_specs += [pl.BlockSpec(memory_space=pltpu.HBM)] * 6
             out_shape = [jax.ShapeDtypeStruct((seq_count, count, size, B), jnp.bfloat16)]
             out_specs = [pl.BlockSpec((seq_count, 1, size, B), lambda i: (0, i, 0, 0))]
             scratch.append(pltpu.VMEM((A, LANES), jnp.float32))
+            scratch += [pltpu.VMEM(arg.shape, arg.dtype) for arg in args[2:]] + [pltpu.SemaphoreType.DMA((6,))]
         else:
             out_shape = [
                 jax.ShapeDtypeStruct((rows, B), jnp.bfloat16),
@@ -399,7 +411,7 @@
         )(*args)
 
     def post(chunk, count, out, coded, *scale):
-        step = min(1024, tok_count)
+        step = min(2048, tok_count)
         block = step // B
         rows = pl.BlockSpec((step, LANES), lambda u, i: (i, chunk + u))
         in_specs = [
@@ -433,7 +445,7 @@
             in_specs=in_specs,
             out_specs=rows,
             out_shape=jax.ShapeDtypeStruct((tok_count, chan_width), jnp.float32),
-            scratch_shapes=[pltpu.VMEM((3, 8, LANES), jnp.float32)],
+            scratch_shapes=[pltpu.VMEM((3, 8 + B, LANES), jnp.float32)],
             input_output_aliases={} if out is None else {len(args) - 1: 0},
             compiler_params=params(),
             cost_estimate=cost(count * 60 * tok_count * LANES, count * 12 * tok_count * LANES),

time: 442 us -> 439 us (level)
  Pallas kernels: 172 us -> 159 us
  waiting for transfers between devices: 222 us -> 232 us
    pallas_call x3, Pallas kernels: 42.7 us -> 33.8 us  [post(): pl.pallas_call(post_parts_kernel if in_parts else post_whole_kernel, grid...]
    all_to_all x3, waiting for transfers between devices: 83.3 us -> 90 us  [per_device(): swap(*conv(start - source, stop - start, coded))]
    pallas_call x2, Pallas kernels: 34.2 us -> 29.2 us  [pre(): pl.pallas_call(partial(pre_parts_kernel, per) if in_parts else pre_whole_...]
  transfers between devices with their start and end apart: 6 -> 6, of which waited for: 4 -> 4; matrix products, arithmetic and copies ran while one was open for 0% -> 0% of each run, Pallas kernels for 34% -> 32%
where the time goes in v3:
time: 439 us; the launch traced here: 437 us
  waiting for transfers between devices  232 us (53%)
  Pallas kernels  159 us (36%)
  starting transfers between devices  29.7 us (7%)
  local copies, waits for them, and re-layouts  14.6 us (3%)
    all_to_all x1, waiting for transfers between devices, per_device(): arrived.append((1, swap(*pre(1, chunks - 1))))  109 us
    pallas_call x3, Pallas kernels, conv(): pl.pallas_call(partial(conv_parts_kernel, per) if in_parts else conv_whol...  92.8 us
    all_to_all x3, waiting for transfers between devices, per_device(): swap(*conv(start - source, stop - start, coded))  90 us
    pallas_call x3, Pallas kernels, post(): pl.pallas_call(post_parts_kernel if in_parts else post_whole_kernel, grid...  33.8 us
    all_to_all x1, waiting for transfers between devices, per_device(): arrived = [(0, swap(*pre(0, 1, own_filter)))]  33.4 us
    pallas_call x2, Pallas kernels, pre(): pl.pallas_call(partial(pre_parts_kernel, per) if in_parts else pre_whole_...  29.2 us
    all_to_all x3, starting transfers between devices, per_device(): swap(*conv(start - source, stop - start, coded))  14 us
    unnamed x41, local copies, waits for them, and re-layouts  13.2 us
  transfers between devices with their start and end apart: 6, of which 4 were waited for; matrix products, arithmetic and copies ran while one was open for 0% of the time, Pallas kernels for 32%

profile of v3, /device:TPU:0, one launch (start us, length us, event | category | flops | bytes accessed | tf_op | source)
XLA Modules:
  0.0 437.2 jit_solution(13051327413708865289)
XLA Ops:
  1.4 4.8 %collective-permute-start = (bf16[3,8,512]{2,1,0:T(8,128)(2,1)S(1)}, bf16[3,8,512]{2,1,0:T(8,128)(2,1)S(1)}, u32[]{:S(2)}, u32[]{:S(2)}) collective-permute-start(bf16[3,8,512]{2,1,0:T(8,128)(2,1)S(1)} %pad_maximum_fusion), channel_id=1, source_target_pairs={{0,1},{1,2},{2,3},{3,4},{4,5},{5,6},{6,7},{8,9},{9,10},{10,11},{11... | collective-permute-start | bytes 73736 | tf_op jit(solution)/shard_map/ppermute | solution.py:343
  6.8 1.5 reduce.3
  9.0 9.2 %pre.3 = bf16[8,1,584,256]{3,2,1,0:T(8,128)(2,1)} custom-call(bf16[8192,512]{1,0:T(8,128)(2,1)} %refs_1_.6, bf16[8192,512]{1,0:T(8,128)(2,1)} %refs_2_.6, bf16[3,8,512]{2,1,0:T(8,128)(2,1)S(1)} %collective-permute-done.halo_ref.refs_3_, f32[3,3,512]{2,1,0:T(4,128)S(1)} %copy-done.13, f32[32,256]{1,0:T(8,128)S(1)} %reshape.7.rest_0_), custom_call_target="tpu_custom_call" | custom-call | flops 41943 | bytes 6291 | tf_op jit(solution)/shard_map/pre/pallas_call | solution.py:363
  18.2 6.1 %all-to-all-start.1 = ((bf16[8,1,584,256]{3,2,1,0:T(8,128)(2,1)}), bf16[8,1,584,256]{3,2,1,0:T(8,128)(2,1)}, u32[]{:S(2)}, u32[]{:S(2)}) async-start(bf16[8,1,584,256]{3,2,1,0:T(8,128)(2,1)} %pre.3), calls=%async_computation.1 | async-start | bytes 4784128 | tf_op jit(solution)/shard_map/all_to_all | solution.py:457
  24.3 20.1 %pre.2 = bf16[8,3,520,256]{3,2,1,0:T(8,128)(2,1)} custom-call(bf16[8192,512]{1,0:T(8,128)(2,1)} %refs_1_.6, bf16[8192,512]{1,0:T(8,128)(2,1)} %refs_2_.6, bf16[3,8,512]{2,1,0:T(8,128)(2,1)S(1)} %collective-permute-done.halo_ref.refs_3_, f32[3,3,512]{2,1,0:T(4,128)S(1)} %copy-done.14), custom_call_target="tpu_custom_call" | custom-call | flops 125829 | bytes 18874 | tf_op jit(solution)/shard_map/pre/pallas_call | solution.py:363
  44.4 33.4 %all-to-all-done.1.parts_ref = bf16[8,1,584,256]{3,2,1,0:T(8,128)(2,1)} async-done(((bf16[8,1,584,256]{3,2,1,0:T(8,128)(2,1)}), bf16[8,1,584,256]{3,2,1,0:T(8,128)(2,1)}, u32[]{:S(2)}, u32[]{:S(2)}) %all-to-all-start.1) | async-done | bytes 2392096 | tf_op jit(solution)/shard_map/all_to_all | solution.py:457
  77.8 4.8 %all-to-all-start = ((bf16[8,3,520,256]{3,2,1,0:T(8,128)(2,1)}), bf16[8,3,520,256]{3,2,1,0:T(8,128)(2,1)}, u32[]{:S(2)}, u32[]{:S(2)}) async-start(bf16[8,3,520,256]{3,2,1,0:T(8,128)(2,1)} %pre.2), calls=%async_computation | async-start | bytes 12779520 | tf_op jit(solution)/shard_map/all_to_all | solution.py:459
  82.6 2.9 spectrum.1
  85.5 23.4 %conv.5 = bf16[8,1,520,256]{3,2,1,0:T(8,128)(2,1)S(1)} custom-call(s32[1]{0:T(128)} %bitcast.4.place_ref, bf16[8,1,584,256]{3,2,1,0:T(8,128)(2,1)} %all-to-all-done.1.parts_ref, bf16[512,768]{1,0:T(8,128)(2,1)S(1)} %get-tuple-element.9.rest_0_, bf16[1536,512]{1,0:T(8,128)(2,1)S(1)} %get-tuple-element.10.rest_1_, f32[256,256]{1,0:T(8,128)S(1)} %copy-done.6, ...), custom_call_target="tpu_custom_call" | custom-call | flops 12884901 | bytes 4194 | tf_op jit(solution)/shard_map/conv/pallas_call | solution.py:401
  110.1 1.4 copy-done.4
  112.9 109.0 %all-to-all-done.parts_ref = bf16[8,3,520,256]{3,2,1,0:T(8,128)(2,1)} async-done(((bf16[8,3,520,256]{3,2,1,0:T(8,128)(2,1)}), bf16[8,3,520,256]{3,2,1,0:T(8,128)(2,1)}, u32[]{:S(2)}, u32[]{:S(2)}) %all-to-all-start) | async-done | bytes 6389792 | tf_op jit(solution)/shard_map/all_to_all | solution.py:459
  221.9 3.6 all-to-all-start.4
  225.6 1.4 copy-done.1
  228.9 46.1 %conv.4 = bf16[8,2,520,256]{3,2,1,0:T(8,128)(2,1)} custom-call(s32[1]{0:T(128)} %bitcast.4.place_ref, bf16[8,3,520,256]{3,2,1,0:T(8,128)(2,1)} %all-to-all-done.parts_ref, bf16[512,768]{1,0:T(8,128)(2,1)S(1)} %get-tuple-element.9.rest_0_, bf16[1536,512]{1,0:T(8,128)(2,1)S(1)} %copy-done.1, f32[256,256]{1,0:T(8,128)S(1)} %copy-done.6, ...), custom_call_target="tpu_custom_call" | custom-call | flops 25769804 | bytes 8388 | tf_op jit(solution)/shard_map/conv/pallas_call | solution.py:401
  275.0 6.0 %all-to-all-start.3 = ((bf16[8,2,520,256]{3,2,1,0:T(8,128)(2,1)}), bf16[8,2,520,256]{3,2,1,0:T(8,128)(2,1)}, u32[]{:S(2)}, u32[]{:S(2)}) async-start(bf16[8,2,520,256]{3,2,1,0:T(8,128)(2,1)} %conv.4), calls=%async_computation.3 | async-start | bytes 8519680 | tf_op jit(solution)/shard_map/all_to_all | solution.py:487
  281.1 1.4 copy-done.2
  284.4 23.3 %conv.3 = bf16[8,1,520,256]{3,2,1,0:T(8,128)(2,1)S(1)} custom-call(s32[1]{0:T(128)} %bitcast.4.place_ref, bf16[8,3,520,256]{3,2,1,0:T(8,128)(2,1)} %all-to-all-done.parts_ref, bf16[512,768]{1,0:T(8,128)(2,1)S(1)} %get-tuple-element.9.rest_0_, bf16[1536,512]{1,0:T(8,128)(2,1)S(1)} %copy-done.2, f32[256,256]{1,0:T(8,128)S(1)} %copy-done.6, ...), custom_call_target="tpu_custom_call" | custom-call | flops 12884901 | bytes 4194 | tf_op jit(solution)/shard_map/conv/pallas_call | solution.py:401
  307.7 1.3 copy-done.3
  309.0 66.2 %all-to-all-done.3.refs_6_.refs_7_ = bf16[8,2,520,256]{3,2,1,0:T(8,128)(2,1)} async-done(((bf16[8,2,520,256]{3,2,1,0:T(8,128)(2,1)}), bf16[8,2,520,256]{3,2,1,0:T(8,128)(2,1)}, u32[]{:S(2)}, u32[]{:S(2)}) %all-to-all-start.3) | async-done | bytes 4259872 | tf_op jit(solution)/shard_map/all_to_all | solution.py:487
  375.3 4.4 all-to-all-start.2
  379.6 8.7 %post.3.refs_8_ = f32[8192,512]{1,0:T(8,128)} custom-call(bf16[8192,512]{1,0:T(8,128)(2,1)} %refs_0_.6, bf16[8192,512]{1,0:T(8,128)(2,1)} %refs_1_.6, bf16[8192,512]{1,0:T(8,128)(2,1)} %refs_2_.6, bf16[3,8,512]{2,1,0:T(8,128)(2,1)S(1)} %collective-permute-done.halo_ref.refs_3_, f32[3,3,512]{2,1,0:T(4,128)S(1)} %copy-done.14, f32[1,512]{1,0:T(1,128)S(1)} %bitcast.8, ...), custom_call_target="tpu_custom_call" | custom-call | flops 62914 | bytes 12582 | tf_op jit(solution)/shard_map/post/pallas_call | solution.py:442
  388.4 16.0 %post.4.refs_8_ = f32[8192,512]{1,0:T(8,128)} custom-call(bf16[8192,512]{1,0:T(8,128)(2,1)} %refs_0_.6, bf16[8192,512]{1,0:T(8,128)(2,1)} %refs_1_.6, bf16[8192,512]{1,0:T(8,128)(2,1)} %refs_2_.6, bf16[3,8,512]{2,1,0:T(8,128)(2,1)S(1)} %collective-permute-done.halo_ref.refs_3_, f32[3,3,512]{2,1,0:T(4,128)S(1)} %copy-done.14, ...), custom_call_target="tpu_custom_call", output_to_operand_aliasing={{}: (8, {})} | custom-call | flops 125829 | bytes 25165 | tf_op jit(solution)/shard_map/post/pallas_call | solution.py:442
  404.4 23.7 %all-to-all-done.2.refs_6_.refs_7_ = bf16[8,1,520,256]{3,2,1,0:T(8,128)(2,1)} async-done(((bf16[8,1,520,256]{3,2,1,0:T(8,128)(2,1)}), bf16[8,1,520,256]{3,2,1,0:T(8,128)(2,1)}, u32[]{:S(2)}, u32[]{:S(2)}) %all-to-all-start.2) | async-done | bytes 2129952 | tf_op jit(solution)/shard_map/all_to_all | solution.py:487
  428.2 9.1 %post.5 = f32[8192,512]{1,0:T(8,128)} custom-call(bf16[8192,512]{1,0:T(8,128)(2,1)} %refs_0_.6, bf16[8192,512]{1,0:T(8,128)(2,1)} %refs_1_.6, bf16[8192,512]{1,0:T(8,128)(2,1)} %refs_2_.6, bf16[3,8,512]{2,1,0:T(8,128)(2,1)S(1)} %collective-permute-done.halo_ref.refs_3_, f32[3,3,512]{2,1,0:T(4,128)S(1)} %copy-done.14, ...), custom_call_target="tpu_custom_call", output_to_operand_aliasing={{}: (8, {})} | custom-call | flops 62914 | bytes 12582 | tf_op jit(solution)/shard_map/post/pallas_call | solution.py:442
  (43 shorter events, 9.1 us)
Async XLA Ops:
  1.4 6.9 %collective-permute-start = (bf16[3,8,512]{2,1,0:T(8,128)(2,1)S(1)}, bf16[3,8,512]{2,1,0:T(8,128)(2,1)S(1)}, u32[]{:S(2)}, u32[]{:S(2)}) collective-permute-start(bf16[3,8,512]{2,1,0:T(8,128)(2,1)S(1)} %pad_maximum_fusion), channel_id=1, source_target_pairs={{0,1},{1,2},{2,3},{3,4},{4,5},{5,6},{6,7},{8,9},{9,10},{10,11},{11... | collective-permute-start | bytes 73736 | tf_op jit(solution)/shard_map/ppermute | solution.py:343
  8.3 0.7 copy-start.13
  9.0 15.3 %copy-start.14 = (f32[3,3,512]{2,1,0:T(4,128)S(1)}, f32[3,3,512]{2,1,0:T(4,128)}, u32[]{:S(2)}) copy-start(f32[3,3,512]{2,1,0:T(4,128)} %refs_4_.6) | copy-start | bytes 55300
  18.2 59.6 %all-to-all-start.1 = ((bf16[8,1,584,256]{3,2,1,0:T(8,128)(2,1)}), bf16[8,1,584,256]{3,2,1,0:T(8,128)(2,1)}, u32[]{:S(2)}, u32[]{:S(2)}) async-start(bf16[8,1,584,256]{3,2,1,0:T(8,128)(2,1)} %pre.3), calls=%async_computation.1 | async-start | bytes 4784128 | tf_op jit(solution)/shard_map/all_to_all | solution.py:457
  44.3 38.2 %copy-start.5 = (f32[256,256]{1,0:T(8,128)S(1)}, f32[256,256]{1,0:T(8,128)}, u32[]{:S(2)}) copy-start(f32[256,256]{1,0:T(8,128)} %constant.21.clone.refs_5_.rest_3_) | copy-start | bytes 786436
  44.3 38.3 %copy-start.6 = (f32[256,256]{1,0:T(8,128)S(1)}, f32[256,256]{1,0:T(8,128)}, u32[]{:S(2)}) copy-start(f32[256,256]{1,0:T(8,128)} %constant.20.clone.refs_4_.rest_2_) | copy-start | bytes 786436
  44.3 38.3 %copy-start.15 = (bf16[256,256]{1,0:T(8,128)(2,1)S(1)}, bf16[256,256]{1,0:T(8,128)(2,1)}, u32[]{:S(2)}) copy-start(bf16[256,256]{1,0:T(8,128)(2,1)} %constant.19.clone.refs_3_) | copy-start | bytes 393220
  44.3 38.3 %copy-start.16 = (bf16[256,256]{1,0:T(8,128)(2,1)S(1)}, bf16[256,256]{1,0:T(8,128)(2,1)}, u32[]{:S(2)}) copy-start(bf16[256,256]{1,0:T(8,128)(2,1)} %constant.18.clone.refs_2_) | copy-start | bytes 393220
  44.4 38.3 %copy-start.17 = (bf16[256,256]{1,0:T(8,128)(2,1)S(1)}, bf16[256,256]{1,0:T(8,128)(2,1)}, u32[]{:S(2)}) copy-start(bf16[256,256]{1,0:T(8,128)(2,1)} %constant.17.clone.refs_1_) | copy-start | bytes 393220
  44.4 38.3 %copy-start.18 = (bf16[256,256]{1,0:T(8,128)(2,1)S(1)}, bf16[256,256]{1,0:T(8,128)(2,1)}, u32[]{:S(2)}) copy-start(bf16[256,256]{1,0:T(8,128)(2,1)} %constant.16.clone.refs_0_) | copy-start | bytes 393220
  77.8 144.2 %all-to-all-start = ((bf16[8,3,520,256]{3,2,1,0:T(8,128)(2,1)}), bf16[8,3,520,256]{3,2,1,0:T(8,128)(2,1)}, u32[]{:S(2)}, u32[]{:S(2)}) async-start(bf16[8,3,520,256]{3,2,1,0:T(8,128)(2,1)} %pre.2), calls=%async_computation | async-start | bytes 12779520 | tf_op jit(solution)/shard_map/all_to_all | solution.py:459
  108.9 1.2 copy-start
  110.1 1.4 copy-start.4
  221.9 53.1 %all-to-all-start.4 = ((bf16[8,1,520,256]{3,2,1,0:T(8,128)(2,1)}), bf16[8,1,520,256]{3,2,1,0:T(8,128)(2,1)S(1)}, u32[]{:S(2)}, u32[]{:S(2)}) async-start(bf16[8,1,520,256]{3,2,1,0:T(8,128)(2,1)} %copy-done.4), calls=%async_computation.4 | async-start | bytes 4259840 | tf_op jit(solution)/shard_map/all_to_all | solution.py:487
  225.6 1.4 copy-start.1
  227.0 0.9 copy-start.8
  227.9 0.9 copy-start.11
  275.0 100.2 %all-to-all-start.3 = ((bf16[8,2,520,256]{3,2,1,0:T(8,128)(2,1)}), bf16[8,2,520,256]{3,2,1,0:T(8,128)(2,1)}, u32[]{:S(2)}, u32[]{:S(2)}) async-start(bf16[8,2,520,256]{3,2,1,0:T(8,128)(2,1)} %conv.4), calls=%async_computation.3 | async-start | bytes 8519680 | tf_op jit(solution)/shard_map/all_to_all | solution.py:487
  281.1 1.4 copy-start.2
  282.5 0.9 copy-start.9
  283.4 0.9 copy-start.12
  284.4 95.3 %copy-start.19 = (f32[512]{0:T(512)S(1)}, f32[512]{0:T(512)}, u32[]{:S(2)}) copy-start(f32[512]{0:T(512)} %param.16) | copy-start | bytes 6148
  307.7 1.3 copy-start.3
  375.3 52.9 %all-to-all-start.2 = ((bf16[8,1,520,256]{3,2,1,0:T(8,128)(2,1)}), bf16[8,1,520,256]{3,2,1,0:T(8,128)(2,1)}, u32[]{:S(2)}, u32[]{:S(2)}) async-start(bf16[8,1,520,256]{3,2,1,0:T(8,128)(2,1)} %copy-done.3), calls=%async_computation.2 | async-start | bytes 4259840 | tf_op jit(solution)/shard_map/all_to_all | solution.py:487
  (2 other events, 1.4 us)

commit v4 on v3

--- a/solution.py
+++ b/solution.py
@@ -84,7 +84,8 @@
 def gate_all(key_ref, value_ref, halo_ref, taps_ref, gated_ref, window_ref):
     taps = taps_ref[...]
     for which in range(1, 3):
-        window_ref[which, B:, :] = halo_ref[which].astype(jnp.float32)
+        before = jnp.zeros((8, LANES), jnp.float32) if halo_ref is None else halo_ref[which].astype(jnp.float32)
+        window_ref[which, B:, :] = before
 
     def gate(slab, most):
         rows = pl.ds(pl.multiple_of(slab * B, B), B)
@@ -106,6 +107,27 @@
     return jnp.broadcast_to(jnp.concatenate([scale, scale], axis=1), (EXTRA, B)).astype(jnp.bfloat16)
 
 
+def edges(key_ref, value_ref):
+    row = lax.broadcasted_iota(jnp.int32, (8, LANES), 0)
+    key_first, value_first = (ref[:8, :].astype(jnp.float32) for ref in (key_ref, value_ref))
+    key_last, value_last = (ref[ref.shape[0] - 8 :, :].astype(jnp.float32) for ref in (key_ref, value_ref))
+    firsts = jnp.where(row < 2, key_first, pltpu.roll(value_first, 4, axis=0))
+    lasts = jnp.where(row < 6, pltpu.roll(key_last, 4, axis=0), value_last)
+    return jnp.where((row < 2) | ((row >= 4) & (row < 6)), firsts, lasts)
+
+
+def edge_gated(mine, before, taps):
+    result = []
+    for position in range(2):
+        pair = []
+        for which in range(2):
+            base = 4 * which
+            lines = [before[base + 2 : base + 3], before[base + 3 : base + 4], mine[base : base + 1], mine[base + 1 : base + 2]]
+            pair.append(sum(taps[tap, 1 + which][None, :] * lines[2 + position - tap] for tap in range(3)))
+        result.append(pair[0] * pair[1])
+    return result
+
+
 def pre_whole_kernel(key_ref, value_ref, halo_ref, taps_ref, coded_ref, scale_ref, gated_ref, window_ref):
     scale = gate_all(key_ref, value_ref, halo_ref, taps_ref, gated_ref, window_ref)
     scale_ref[...] = scale
@@ -119,11 +141,11 @@
     lax.fori_loop(0, coded_ref.shape[0], send, 0)
 
 
-def pre_parts_kernel(per, key_ref, value_ref, halo_ref, taps_ref, *rest):
-    filter_refs, (parts_ref, gated_ref, window_ref) = rest[:-3], rest[-3:]
+def pre_parts_kernel(per, key_ref, value_ref, taps_ref, *rest):
+    filter_refs, (parts_ref, gated_ref, window_ref, filter_rows_ref) = rest[:-4], rest[-4:]
     count, _, size, _ = parts_ref.shape
     slabs = key_ref.shape[0] // B
-    scale = gate_all(key_ref, value_ref, halo_ref, taps_ref, gated_ref, window_ref)
+    scale = gate_all(key_ref, value_ref, None, taps_ref, gated_ref, window_ref)
     factor = 1.0 / scale
 
     def send(slab, _):
@@ -135,10 +157,14 @@
         return 0
 
     lax.fori_loop(0, slabs, send, 0)
-    tile = scale_tile(scale)
+    tile = jnp.concatenate([jnp.broadcast_to(scale, (EXTRA, LANES)), edges(key_ref, value_ref)], axis=1).astype(jnp.bfloat16)
+    for filter_ref in filter_refs:
+        for slab in range(slabs):
+            filter_rows_ref[slab : slab + 1, :] = filter_ref[:, slab * B : (slab + 1) * B]
+        filter_rows = jnp.concatenate(split(filter_rows_ref[...]), axis=0)
+        for target in range(count):
+            parts_ref[target, 0, slabs * per : size - EXTRA, :] = filter_rows
     for target in range(count):
-        for filter_ref in filter_refs:
-            parts_ref[target, 0, slabs * per : size - EXTRA, :] = jnp.concatenate(split(filter_ref[...]), axis=0)
         parts_ref[target, 0, size - EXTRA :, :] = tile
 
 
@@ -230,8 +256,8 @@
     lax.fori_loop(0, per, send, 0)
 
 
-def conv_parts_kernel(per, place_ref, parts_ref, *rest):
-    sources, (out_ref, work_ref, scale_ref), constants, sems = rest[:6], rest[6:9], rest[9:15], rest[15]
+def conv_parts_kernel(per, place_ref, parts_ref, taps_ref, *rest):
+    sources, (out_ref, work_ref, scale_ref, edge_ref), constants, sems = rest[:6], rest[6:10], rest[10:16], rest[16]
     copies = [pltpu.make_async_copy(*pair, sems.at[index]) for index, pair in enumerate(zip(sources, constants))]
 
     @pl.when(pl.program_id(0) == 0)
@@ -254,6 +280,23 @@
         return 0
 
     lax.fori_loop(0, count, receive, 0)
+
+    taps = taps_ref[...]
+    edge_ref[...] = jnp.zeros_like(edge_ref)
+    before = jnp.zeros((EXTRA, LANES), jnp.float32)
+    for index in range(count):
+        end = parts_ref[index, 0, size - EXTRA :, :].astype(jnp.float32)
+        mine = end[:, LANES:]
+        for position, gated in enumerate(edge_gated(mine, before, taps)):
+            edge_ref[2 * index + position : 2 * index + position + 1, :] = gated / end[:1, :LANES]
+        before = mine
+    edge_ref[...] = edge_ref[...].T
+    fixed = edge_ref[pl.ds(pl.multiple_of(place_ref[0] * per, per), per), :]
+    lane = lax.broadcasted_iota(jnp.int32, (per, LANES), 1)
+    for index in range(count):
+        rows = slice(index * block, index * block + per)
+        moved = pltpu.roll(fixed, (LANES - 2 * index) % LANES, axis=1)
+        work_ref[0, rows, :] = jnp.where(lane < 2, moved, work_ref[0, rows, :])
 
     @pl.when(pl.program_id(0) == 0)
     def _():
@@ -363,35 +406,34 @@
         return pl.pallas_call(
             partial(pre_parts_kernel, per) if in_parts else pre_whole_kernel,
             grid=(count,),
-            in_specs=[
-                rows,
-                rows,
-                pl.BlockSpec((3, 8, LANES), lambda i: (0, 0, chunk + i)),
-                pl.BlockSpec((3, 3, LANES), lambda i: (0, 0, chunk + i)),
-            ]
-            + [whole_block((slabs, B))] * len(filters),
+            in_specs=[rows, rows]
+            + [pl.BlockSpec((3, 8, LANES), lambda i: (0, 0, chunk + i))] * (not in_parts)
+            + [pl.BlockSpec((3, 3, LANES), lambda i: (0, 0, chunk + i))]
+            + [whole_block((1, tok_count))] * len(filters),
             out_specs=out_specs,
             out_shape=out_shape,
-            scratch_shapes=[pltpu.VMEM((tok_count, LANES), jnp.float32), pltpu.VMEM((3, 8 + B, LANES), jnp.float32)],
+            scratch_shapes=[pltpu.VMEM((tok_count, LANES), jnp.float32), pltpu.VMEM((3, 8 + B, LANES), jnp.float32)]
+            + [pltpu.VMEM((slabs, B), jnp.float32)] * in_parts,
             compiler_params=params(),
             cost_estimate=cost(count * 40 * tok_count * LANES, count * 6 * tok_count * LANES),
             name="pre",
-        )(key_proj, value_proj, halo, short_taps, *filters)
-
-    def conv(first, count, coded, *scale):
+        )(key_proj, value_proj, *[halo] * (not in_parts), short_taps, *filters)
+
+    def conv(start, first, count, coded, *scale):
         rows = A * per
         args = (coded, *scale, left, right, turn_re, turn_im, spec_re, spec_im)
         in_specs = [whole_block(arg.shape) for arg in args]
         scratch = [pltpu.VMEM((2, rows, LANES), jnp.float32)]
         if in_parts:
-            args = (place,) + args
+            args = (place, coded, short_taps) + args[1:]
             block = (seq_count, 1, coded.shape[2], B)
             in_specs = [SCALAR, pl.BlockSpec(block, lambda i: (0, first + i, 0, 0))]
+            in_specs.append(pl.BlockSpec((3, 3, LANES), lambda i: (0, 0, start + i)))
             in_specs += [pl.BlockSpec(memory_space=pltpu.HBM)] * 6
             out_shape = [jax.ShapeDtypeStruct((seq_count, count, size, B), jnp.bfloat16)]
             out_specs = [pl.BlockSpec((seq_count, 1, size, B), lambda i: (0, i, 0, 0))]
-            scratch.append(pltpu.VMEM((A, LANES), jnp.float32))
-            scratch += [pltpu.VMEM(arg.shape, arg.dtype) for arg in args[2:]] + [pltpu.SemaphoreType.DMA((6,))]
+            scratch += [pltpu.VMEM((A, LANES), jnp.float32), pltpu.VMEM((LANES, LANES), jnp.float32)]
+            scratch += [pltpu.VMEM(arg.shape, arg.dtype) for arg in args[3:]] + [pltpu.SemaphoreType.DMA((6,))]
         else:
             out_shape = [
                 jax.ShapeDtypeStruct((rows, B), jnp.bfloat16),
@@ -452,15 +494,14 @@
             name="post",
         )(*args)
 
-    own_filter = long_filter.reshape(slabs, B)
     if in_parts:
-        arrived = [(0, swap(*pre(0, 1, own_filter)))]
+        arrived = [(0, swap(*pre(0, 1, long_filter)))]
         if chunks > 1:
             arrived.append((1, swap(*pre(1, chunks - 1))))
         whole_filter = arrived[0][1]
         filter_spec = pl.BlockSpec((seq_count, 1, 2 * slabs, B), lambda i: (0, 0, per // 2, 0))
     else:
-        whole_filter = swap(jnp.broadcast_to(own_filter, (seq_count, slabs, B))).reshape(A, B)
+        whole_filter = swap(jnp.broadcast_to(long_filter.reshape(slabs, B), (seq_count, slabs, B))).reshape(A, B)
         filter_spec = whole_block((A, B))
     cos_hi, sin_hi, cos_lo, sin_lo, turn_re, turn_im = (jnp.asarray(table) for table in tables())
     filter_args = (whole_filter, cos_hi, sin_hi, cos_lo, sin_lo, turn_re, turn_im)
@@ -484,7 +525,10 @@
         returned = []
         for start, stop in zip(cuts[:-1], cuts[1:]):
             source, coded = arrived[min(start, 1)]
-            returned.append((start, stop - start, swap(*conv(start - source, stop - start, coded))))
+            (coded,) = conv(start, start - source, stop - start, coded)
+            if start == 0:
+                coded, halo = lax.optimization_barrier((coded, halo))
+            returned.append((start, stop - start, swap(coded)))
         for start, count, coded in returned:
             out = post(start, count, out, coded)
     else:
@@ -494,7 +538,7 @@
             coded = swap(coded.reshape(slabs, seq_count, per, B).transpose(1, 0, 2, 3))
             scale = jnp.repeat(swap(scale.reshape(seq_count, per)), slabs, axis=0)
             scale = jnp.pad(scale, ((0, 0), (0, LANES - per)))
-            coded, scale = conv(0, 1, coded.reshape(A * per, B), scale)
+            coded, scale = conv(chunk, 0, 1, coded.reshape(A * per, B), scale)
             coded = swap(coded.reshape(seq_count, slabs, per, B))
             scale = lax.all_gather(scale[0, :per], "seq", axis=0, tiled=True)
             returned.append((coded.transpose(1, 0, 2, 3).reshape(slabs, LANES, B), scale.reshape(1, LANES)))

time: 439 us -> 434 us (0.989)
    all_to_all x1, waiting for transfers between devices: 109 us -> 87.7 us  [per_device(): arrived.append((1, swap(*pre(1, chunks - 1))))]
    ppermute x1, waiting for transfers between devices: 0.01 us -> 17 us  [per_device(): lax.ppermute(ends, 'seq', [(source, source + 1) for source in range(seq_c...]
    unnamed x41 -> x42, local copies, waits for them, and re-layouts: 13.2 us -> 12.1 us
  transfers between devices with their start and end apart: 6 -> 6, of which waited for: 4 -> 5; matrix products, arithmetic and copies ran while one was open for 0% -> 0% of each run, Pallas kernels for 32% -> 33%
where the time goes in v4:
time: 434 us; the launch traced here: 433 us
  waiting for transfers between devices  229 us (53%)
  Pallas kernels  160 us (37%)
  starting transfers between devices  30 us (7%)
  local copies, waits for them, and re-layouts  13.5 us (3%)
    pallas_call x3, Pallas kernels, conv(): pl.pallas_call(partial(conv_parts_kernel, per) if in_parts else conv_whol...  94.3 us
    all_to_all x3, waiting for transfers between devices, per_device(): returned.append((start, stop - start, swap(coded)))  89.5 us
    all_to_all x1, waiting for transfers between devices, per_device(): arrived.append((1, swap(*pre(1, chunks - 1))))  87.7 us
    all_to_all x1, waiting for transfers between devices, per_device(): arrived = [(0, swap(*pre(0, 1, long_filter)))]  34.6 us
    pallas_call x3, Pallas kernels, post(): pl.pallas_call(post_parts_kernel if in_parts else post_whole_kernel, grid...  33.8 us
    pallas_call x2, Pallas kernels, pre(): pl.pallas_call(partial(pre_parts_kernel, per) if in_parts else pre_whole_...  29.1 us
    ppermute x1, waiting for transfers between devices, per_device(): lax.ppermute(ends, 'seq', [(source, source + 1) for source in range(seq_c...  17 us
    all_to_all x3, starting transfers between devices, per_device(): returned.append((start, stop - start, swap(coded)))  14.2 us
  transfers between devices with their start and end apart: 6, of which 5 were waited for; matrix products, arithmetic and copies ran while one was open for 0% of the time, Pallas kernels for 33%

profile of v4, /device:TPU:0, one launch (start us, length us, event | category | flops | bytes accessed | tf_op | source)
XLA Modules:
  0.0 432.8 jit_solution(2517677050311027905)
XLA Ops:
  1.5 9.1 %pre.2 = bf16[8,1,584,256]{3,2,1,0:T(8,128)(2,1)} custom-call(bf16[8192,512]{1,0:T(8,128)(2,1)} %refs_1_.6, bf16[8192,512]{1,0:T(8,128)(2,1)} %refs_2_.6, f32[3,3,512]{2,1,0:T(4,128)S(1)} %copy-done.13, f32[1,8192]{1,0:T(1,128)S(1)} %copy-done.19), custom_call_target="tpu_custom_call" | custom-call | flops 41943 | bytes 6291 | tf_op jit(solution)/shard_map/pre/pallas_call | solution.py:406
  10.6 7.3 %all-to-all-start = ((bf16[8,1,584,256]{3,2,1,0:T(8,128)(2,1)}), bf16[8,1,584,256]{3,2,1,0:T(8,128)(2,1)}, u32[]{:S(2)}, u32[]{:S(2)}) async-start(bf16[8,1,584,256]{3,2,1,0:T(8,128)(2,1)} %pre.2), calls=%async_computation | async-start | bytes 4784128 | tf_op jit(solution)/shard_map/all_to_all | solution.py:498
  17.9 20.0 %pre.3 = bf16[8,3,520,256]{3,2,1,0:T(8,128)(2,1)} custom-call(bf16[8192,512]{1,0:T(8,128)(2,1)} %refs_1_.6, bf16[8192,512]{1,0:T(8,128)(2,1)} %refs_2_.6, f32[3,3,512]{2,1,0:T(4,128)S(1)} %copy-done.14), custom_call_target="tpu_custom_call" | custom-call | flops 125829 | bytes 18874 | tf_op jit(solution)/shard_map/pre/pallas_call | solution.py:406
  37.9 34.6 %all-to-all-done.parts_ref = bf16[8,1,584,256]{3,2,1,0:T(8,128)(2,1)} async-done(((bf16[8,1,584,256]{3,2,1,0:T(8,128)(2,1)}), bf16[8,1,584,256]{3,2,1,0:T(8,128)(2,1)}, u32[]{:S(2)}, u32[]{:S(2)}) %all-to-all-start) | async-done | bytes 2392096 | tf_op jit(solution)/shard_map/all_to_all | solution.py:498
  72.5 4.8 %all-to-all-start.1 = ((bf16[8,3,520,256]{3,2,1,0:T(8,128)(2,1)}), bf16[8,3,520,256]{3,2,1,0:T(8,128)(2,1)}, u32[]{:S(2)}, u32[]{:S(2)}) async-start(bf16[8,3,520,256]{3,2,1,0:T(8,128)(2,1)} %pre.3), calls=%async_computation.1 | async-start | bytes 12779520 | tf_op jit(solution)/shard_map/all_to_all | solution.py:500
  78.7 3.8 collective-permute-start
  82.6 2.9 spectrum.1
  85.5 23.9 %conv.3 = bf16[8,1,520,256]{3,2,1,0:T(8,128)(2,1)S(1)} custom-call(s32[1]{0:T(128)} %bitcast.place_ref, bf16[8,1,584,256]{3,2,1,0:T(8,128)(2,1)} %all-to-all-done.parts_ref, f32[3,3,512]{2,1,0:T(4,128)S(1)} %copy-done.14, bf16[512,768]{1,0:T(8,128)(2,1)S(1)} %get-tuple-element.11.rest_0_, bf16[1536,512]{1,0:T(8,128)(2,1)S(1)} %get-tuple-element.12.rest_1_, ...), custom_call_target="tpu_custom_call" | custom-call | flops 12884901 | bytes 4194 | tf_op jit(solution)/shard_map/conv/pallas_call | solution.py:443
  110.6 1.4 copy-done.3
  112.0 17.0 %collective-permute-done.refs_3_ = bf16[3,8,512]{2,1,0:T(8,128)(2,1)S(1)} collective-permute-done((bf16[3,8,512]{2,1,0:T(8,128)(2,1)S(1)}, bf16[3,8,512]{2,1,0:T(8,128)(2,1)S(1)}, u32[]{:S(2)}, u32[]{:S(2)}) %collective-permute-start) | collective-permute-done | bytes 24608 | tf_op jit(solution)/shard_map/ppermute | solution.py:386
  129.0 87.7 %all-to-all-done.1.parts_ref = bf16[8,3,520,256]{3,2,1,0:T(8,128)(2,1)} async-done(((bf16[8,3,520,256]{3,2,1,0:T(8,128)(2,1)}), bf16[8,3,520,256]{3,2,1,0:T(8,128)(2,1)}, u32[]{:S(2)}, u32[]{:S(2)}) %all-to-all-start.1) | async-done | bytes 6389792 | tf_op jit(solution)/shard_map/all_to_all | solution.py:500
  216.7 3.8 all-to-all-start.4
  220.5 1.4 copy-done.1
  223.8 46.9 %conv.5 = bf16[8,2,520,256]{3,2,1,0:T(8,128)(2,1)} custom-call(s32[1]{0:T(128)} %bitcast.place_ref, bf16[8,3,520,256]{3,2,1,0:T(8,128)(2,1)} %all-to-all-done.1.parts_ref, f32[3,3,512]{2,1,0:T(4,128)S(1)} %copy-done.14, bf16[512,768]{1,0:T(8,128)(2,1)S(1)} %get-tuple-element.11.rest_0_, bf16[1536,512]{1,0:T(8,128)(2,1)S(1)} %copy-done.1, ...), custom_call_target="tpu_custom_call" | custom-call | flops 25769804 | bytes 8388 | tf_op jit(solution)/shard_map/conv/pallas_call | solution.py:443
  270.7 6.0 %all-to-all-start.3 = ((bf16[8,2,520,256]{3,2,1,0:T(8,128)(2,1)}), bf16[8,2,520,256]{3,2,1,0:T(8,128)(2,1)}, u32[]{:S(2)}, u32[]{:S(2)}) async-start(bf16[8,2,520,256]{3,2,1,0:T(8,128)(2,1)} %conv.5), calls=%async_computation.3 | async-start | bytes 8519680 | tf_op jit(solution)/shard_map/all_to_all | solution.py:531
  276.7 1.4 copy-done.2
  280.0 23.6 %conv.4 = bf16[8,1,520,256]{3,2,1,0:T(8,128)(2,1)S(1)} custom-call(s32[1]{0:T(128)} %bitcast.place_ref, bf16[8,3,520,256]{3,2,1,0:T(8,128)(2,1)} %all-to-all-done.1.parts_ref, f32[3,3,512]{2,1,0:T(4,128)S(1)} %copy-done.14, bf16[512,768]{1,0:T(8,128)(2,1)S(1)} %get-tuple-element.11.rest_0_, bf16[1536,512]{1,0:T(8,128)(2,1)S(1)} %copy-done.2, ...), custom_call_target="tpu_custom_call" | custom-call | flops 12884901 | bytes 4194 | tf_op jit(solution)/shard_map/conv/pallas_call | solution.py:443
  303.7 1.3 copy-done.4
  305.0 65.8 %all-to-all-done.3.refs_6_.refs_7_ = bf16[8,2,520,256]{3,2,1,0:T(8,128)(2,1)} async-done(((bf16[8,2,520,256]{3,2,1,0:T(8,128)(2,1)}), bf16[8,2,520,256]{3,2,1,0:T(8,128)(2,1)}, u32[]{:S(2)}, u32[]{:S(2)}) %all-to-all-start.3) | async-done | bytes 4259872 | tf_op jit(solution)/shard_map/all_to_all | solution.py:531
  370.8 4.3 %all-to-all-start.2 = ((bf16[8,1,520,256]{3,2,1,0:T(8,128)(2,1)}), bf16[8,1,520,256]{3,2,1,0:T(8,128)(2,1)}, u32[]{:S(2)}, u32[]{:S(2)}) async-start(bf16[8,1,520,256]{3,2,1,0:T(8,128)(2,1)} %copy-done.4), calls=%async_computation.2 | async-start | bytes 4259840 | tf_op jit(solution)/shard_map/all_to_all | solution.py:531
  375.2 8.7 %post.3.refs_8_ = f32[8192,512]{1,0:T(8,128)} custom-call(bf16[8192,512]{1,0:T(8,128)(2,1)} %refs_0_.6, bf16[8192,512]{1,0:T(8,128)(2,1)} %refs_1_.6, bf16[8192,512]{1,0:T(8,128)(2,1)} %refs_2_.6, bf16[3,8,512]{2,1,0:T(8,128)(2,1)S(1)} %collective-permute-done.refs_3_, f32[3,3,512]{2,1,0:T(4,128)S(1)} %copy-done.14, f32[1,512]{1,0:T(1,128)S(1)} %bitcast.8, ...), custom_call_target="tpu_custom_call" | custom-call | flops 62914 | bytes 12582 | tf_op jit(solution)/shard_map/post/pallas_call | solution.py:484
  383.9 16.0 %post.4.refs_8_ = f32[8192,512]{1,0:T(8,128)} custom-call(bf16[8192,512]{1,0:T(8,128)(2,1)} %refs_0_.6, bf16[8192,512]{1,0:T(8,128)(2,1)} %refs_1_.6, bf16[8192,512]{1,0:T(8,128)(2,1)} %refs_2_.6, bf16[3,8,512]{2,1,0:T(8,128)(2,1)S(1)} %collective-permute-done.refs_3_, f32[3,3,512]{2,1,0:T(4,128)S(1)} %copy-done.14, ...), custom_call_target="tpu_custom_call", output_to_operand_aliasing={{}: (8, {})} | custom-call | flops 125829 | bytes 25165 | tf_op jit(solution)/shard_map/post/pallas_call | solution.py:484
  399.9 23.8 %all-to-all-done.2.refs_6_.refs_7_ = bf16[8,1,520,256]{3,2,1,0:T(8,128)(2,1)} async-done(((bf16[8,1,520,256]{3,2,1,0:T(8,128)(2,1)}), bf16[8,1,520,256]{3,2,1,0:T(8,128)(2,1)}, u32[]{:S(2)}, u32[]{:S(2)}) %all-to-all-start.2) | async-done | bytes 2129952 | tf_op jit(solution)/shard_map/all_to_all | solution.py:531
  423.7 9.1 %post.5 = f32[8192,512]{1,0:T(8,128)} custom-call(bf16[8192,512]{1,0:T(8,128)(2,1)} %refs_0_.6, bf16[8192,512]{1,0:T(8,128)(2,1)} %refs_1_.6, bf16[8192,512]{1,0:T(8,128)(2,1)} %refs_2_.6, bf16[3,8,512]{2,1,0:T(8,128)(2,1)S(1)} %collective-permute-done.refs_3_, f32[3,3,512]{2,1,0:T(4,128)S(1)} %copy-done.14, ...), custom_call_target="tpu_custom_call", output_to_operand_aliasing={{}: (8, {})} | custom-call | flops 62914 | bytes 12582 | tf_op jit(solution)/shard_map/post/pallas_call | solution.py:484
  (42 shorter events, 7.9 us)
Async XLA Ops:
  1.5 16.4 %copy-start.14 = (f32[3,3,512]{2,1,0:T(4,128)S(1)}, f32[3,3,512]{2,1,0:T(4,128)}, u32[]{:S(2)}) copy-start(f32[3,3,512]{2,1,0:T(4,128)} %refs_4_.6) | copy-start | bytes 55300
  10.6 61.9 %all-to-all-start = ((bf16[8,1,584,256]{3,2,1,0:T(8,128)(2,1)}), bf16[8,1,584,256]{3,2,1,0:T(8,128)(2,1)}, u32[]{:S(2)}, u32[]{:S(2)}) async-start(bf16[8,1,584,256]{3,2,1,0:T(8,128)(2,1)} %pre.2), calls=%async_computation | async-start | bytes 4784128 | tf_op jit(solution)/shard_map/all_to_all | solution.py:498
  37.9 44.7 %copy-start.5 = (f32[256,256]{1,0:T(8,128)S(1)}, f32[256,256]{1,0:T(8,128)}, u32[]{:S(2)}) copy-start(f32[256,256]{1,0:T(8,128)} %constant.21.clone.refs_5_.rest_3_) | copy-start | bytes 786436
  37.9 44.7 %copy-start.6 = (f32[256,256]{1,0:T(8,128)S(1)}, f32[256,256]{1,0:T(8,128)}, u32[]{:S(2)}) copy-start(f32[256,256]{1,0:T(8,128)} %constant.20.clone.refs_4_.rest_2_) | copy-start | bytes 786436
  37.9 44.7 %copy-start.15 = (bf16[256,256]{1,0:T(8,128)(2,1)S(1)}, bf16[256,256]{1,0:T(8,128)(2,1)}, u32[]{:S(2)}) copy-start(bf16[256,256]{1,0:T(8,128)(2,1)} %constant.19.clone.refs_3_) | copy-start | bytes 393220
  37.9 44.7 %copy-start.16 = (bf16[256,256]{1,0:T(8,128)(2,1)S(1)}, bf16[256,256]{1,0:T(8,128)(2,1)}, u32[]{:S(2)}) copy-start(bf16[256,256]{1,0:T(8,128)(2,1)} %constant.18.clone.refs_2_) | copy-start | bytes 393220
  37.9 44.7 %copy-start.17 = (bf16[256,256]{1,0:T(8,128)(2,1)S(1)}, bf16[256,256]{1,0:T(8,128)(2,1)}, u32[]{:S(2)}) copy-start(bf16[256,256]{1,0:T(8,128)(2,1)} %constant.17.clone.refs_1_) | copy-start | bytes 393220
  37.9 44.7 %copy-start.18 = (bf16[256,256]{1,0:T(8,128)(2,1)S(1)}, bf16[256,256]{1,0:T(8,128)(2,1)}, u32[]{:S(2)}) copy-start(bf16[256,256]{1,0:T(8,128)(2,1)} %constant.16.clone.refs_0_) | copy-start | bytes 393220
  72.5 144.2 %all-to-all-start.1 = ((bf16[8,3,520,256]{3,2,1,0:T(8,128)(2,1)}), bf16[8,3,520,256]{3,2,1,0:T(8,128)(2,1)}, u32[]{:S(2)}, u32[]{:S(2)}) async-start(bf16[8,3,520,256]{3,2,1,0:T(8,128)(2,1)} %pre.3), calls=%async_computation.1 | async-start | bytes 12779520 | tf_op jit(solution)/shard_map/all_to_all | solution.py:500
  78.7 50.3 %collective-permute-start = (bf16[3,8,512]{2,1,0:T(8,128)(2,1)S(1)}, bf16[3,8,512]{2,1,0:T(8,128)(2,1)S(1)}, u32[]{:S(2)}, u32[]{:S(2)}) collective-permute-start(bf16[3,8,512]{2,1,0:T(8,128)(2,1)S(1)} %pad_maximum_fusion), channel_id=1, source_target_pairs={{0,1},{1,2},{2,3},{3,4},{4,5},{5,6},{6,7},{8,9},{9,10},{10,11},{11... | collective-permute-start | bytes 73736 | tf_op jit(solution)/shard_map/ppermute | solution.py:386
  85.5 23.9 %copy-start.7 = (f32[256,256]{1,0:T(8,128)}, f32[256,256]{1,0:T(8,128)S(1)}, u32[]{:S(2)}) copy-start(f32[256,256]{1,0:T(8,128)S(1)} %get-tuple-element.13.rest_4_) | copy-start | bytes 786436
  85.5 23.9 %copy-start.10 = (f32[256,256]{1,0:T(8,128)}, f32[256,256]{1,0:T(8,128)S(1)}, u32[]{:S(2)}) copy-start(f32[256,256]{1,0:T(8,128)S(1)} %get-tuple-element.14.rest_5_) | copy-start | bytes 786436
  109.4 1.2 copy-start
  110.6 1.4 copy-start.3
  216.7 54.0 %all-to-all-start.4 = ((bf16[8,1,520,256]{3,2,1,0:T(8,128)(2,1)}), bf16[8,1,520,256]{3,2,1,0:T(8,128)(2,1)S(1)}, u32[]{:S(2)}, u32[]{:S(2)}) async-start(bf16[8,1,520,256]{3,2,1,0:T(8,128)(2,1)} %copy-done.3), calls=%async_computation.4 | async-start | bytes 4259840 | tf_op jit(solution)/shard_map/all_to_all | solution.py:531
  220.5 1.4 copy-start.1
  221.9 0.9 copy-start.8
  222.9 0.9 copy-start.11
  270.7 100.1 %all-to-all-start.3 = ((bf16[8,2,520,256]{3,2,1,0:T(8,128)(2,1)}), bf16[8,2,520,256]{3,2,1,0:T(8,128)(2,1)}, u32[]{:S(2)}, u32[]{:S(2)}) async-start(bf16[8,2,520,256]{3,2,1,0:T(8,128)(2,1)} %conv.5), calls=%async_computation.3 | async-start | bytes 8519680 | tf_op jit(solution)/shard_map/all_to_all | solution.py:531
  276.7 1.4 copy-start.2
  278.1 0.9 copy-start.9
  280.0 95.1 %copy-start.20 = (f32[512]{0:T(512)S(1)}, f32[512]{0:T(512)}, u32[]{:S(2)}) copy-start(f32[512]{0:T(512)} %param.16) | copy-start | bytes 6148
  303.7 1.3 copy-start.4
  370.8 52.9 %all-to-all-start.2 = ((bf16[8,1,520,256]{3,2,1,0:T(8,128)(2,1)}), bf16[8,1,520,256]{3,2,1,0:T(8,128)(2,1)}, u32[]{:S(2)}, u32[]{:S(2)}) async-start(bf16[8,1,520,256]{3,2,1,0:T(8,128)(2,1)} %copy-done.4), calls=%async_computation.2 | async-start | bytes 4259840 | tf_op jit(solution)/shard_map/all_to_all | solution.py:531
  (3 other events, 2.4 us)

commit v5 on v4

--- a/solution.py
+++ b/solution.py
@@ -216,7 +216,7 @@
         put(work_ref, pl.ds(channel, A, stride=per), encode(value * (1.0 / scale)))
         return jnp.where(row_lane == base + channel, scale, scales)
 
-    together = 2 if per % 4 == 0 else 1
+    together = 4 if per % 8 == 0 else 2 if per % 4 == 0 else 1
 
     def convolve(index, scales):
         first = 2 * together * index

time: 434 us -> 431 us (level)
  Pallas kernels: 160 us -> 152 us
  waiting for transfers between devices: 229 us -> 235 us
    pallas_call x3, Pallas kernels: 94.3 us -> 86.1 us  [conv(): pl.pallas_call(partial(conv_parts_kernel, per) if in_parts else conv_whol...]
    all_to_all x3, waiting for transfers between devices: 89.5 us -> 94.1 us  [per_device(): returned.append((start, stop - start, swap(coded)))]
  transfers between devices with their start and end apart: 6 -> 6, of which waited for: 5 -> 6; matrix products, arithmetic and copies ran while one was open for 0% -> 0% of each run, Pallas kernels for 33% -> 31%
where the time goes in v5:
time: 431 us; the launch traced here: 430 us
  waiting for transfers between devices  235 us (55%)
  Pallas kernels  152 us (35%)
  starting transfers between devices  28.8 us (7%)
  local copies, waits for them, and re-layouts  13.5 us (3%)
    all_to_all x3, waiting for transfers between devices, per_device(): returned.append((start, stop - start, swap(coded)))  94.1 us
    all_to_all x1, waiting for transfers between devices, per_device(): arrived.append((1, swap(*pre(1, chunks - 1))))  87.7 us
    pallas_call x3, Pallas kernels, conv(): pl.pallas_call(partial(conv_parts_kernel, per) if in_parts else conv_whol...  86.1 us
    all_to_all x1, waiting for transfers between devices, per_device(): arrived = [(0, swap(*pre(0, 1, long_filter)))]  34.6 us
    pallas_call x3, Pallas kernels, post(): pl.pallas_call(post_parts_kernel if in_parts else post_whole_kernel, grid...  33.8 us
    pallas_call x2, Pallas kernels, pre(): pl.pallas_call(partial(pre_parts_kernel, per) if in_parts else pre_whole_...  29.1 us
    ppermute x1, waiting for transfers between devices, per_device(): lax.ppermute(ends, 'seq', [(source, source + 1) for source in range(seq_c...  19.1 us
    all_to_all x3, starting transfers between devices, per_device(): returned.append((start, stop - start, swap(coded)))  12.9 us
  transfers between devices with their start and end apart: 6, of which 6 were waited for; matrix products, arithmetic and copies ran while one was open for 0% of the time, Pallas kernels for 31%

profile of v5, /device:TPU:0, one launch (start us, length us, event | category | flops | bytes accessed | tf_op | source)
XLA Modules:
  0.0 429.8 jit_solution(14696469297276535844)
XLA Ops:
  1.5 9.1 %pre.2 = bf16[8,1,584,256]{3,2,1,0:T(8,128)(2,1)} custom-call(bf16[8192,512]{1,0:T(8,128)(2,1)} %refs_1_.6, bf16[8192,512]{1,0:T(8,128)(2,1)} %refs_2_.6, f32[3,3,512]{2,1,0:T(4,128)S(1)} %copy-done.13, f32[1,8192]{1,0:T(1,128)S(1)} %copy-done.19), custom_call_target="tpu_custom_call" | custom-call | flops 41943 | bytes 6291 | tf_op jit(solution)/shard_map/pre/pallas_call | solution.py:406
  10.6 7.3 %all-to-all-start = ((bf16[8,1,584,256]{3,2,1,0:T(8,128)(2,1)}), bf16[8,1,584,256]{3,2,1,0:T(8,128)(2,1)}, u32[]{:S(2)}, u32[]{:S(2)}) async-start(bf16[8,1,584,256]{3,2,1,0:T(8,128)(2,1)} %pre.2), calls=%async_computation | async-start | bytes 4784128 | tf_op jit(solution)/shard_map/all_to_all | solution.py:498
  17.9 20.0 %pre.3 = bf16[8,3,520,256]{3,2,1,0:T(8,128)(2,1)} custom-call(bf16[8192,512]{1,0:T(8,128)(2,1)} %refs_1_.6, bf16[8192,512]{1,0:T(8,128)(2,1)} %refs_2_.6, f32[3,3,512]{2,1,0:T(4,128)S(1)} %copy-done.14), custom_call_target="tpu_custom_call" | custom-call | flops 125829 | bytes 18874 | tf_op jit(solution)/shard_map/pre/pallas_call | solution.py:406
  37.9 34.6 %all-to-all-done.parts_ref = bf16[8,1,584,256]{3,2,1,0:T(8,128)(2,1)} async-done(((bf16[8,1,584,256]{3,2,1,0:T(8,128)(2,1)}), bf16[8,1,584,256]{3,2,1,0:T(8,128)(2,1)}, u32[]{:S(2)}, u32[]{:S(2)}) %all-to-all-start) | async-done | bytes 2392096 | tf_op jit(solution)/shard_map/all_to_all | solution.py:498
  72.5 4.8 %all-to-all-start.1 = ((bf16[8,3,520,256]{3,2,1,0:T(8,128)(2,1)}), bf16[8,3,520,256]{3,2,1,0:T(8,128)(2,1)}, u32[]{:S(2)}, u32[]{:S(2)}) async-start(bf16[8,3,520,256]{3,2,1,0:T(8,128)(2,1)} %pre.3), calls=%async_computation.1 | async-start | bytes 12779520 | tf_op jit(solution)/shard_map/all_to_all | solution.py:500
  78.7 3.8 collective-permute-start
  82.6 2.9 spectrum.1
  85.5 21.8 %conv.3 = bf16[8,1,520,256]{3,2,1,0:T(8,128)(2,1)S(1)} custom-call(s32[1]{0:T(128)} %bitcast.place_ref, bf16[8,1,584,256]{3,2,1,0:T(8,128)(2,1)} %all-to-all-done.parts_ref, f32[3,3,512]{2,1,0:T(4,128)S(1)} %copy-done.14, bf16[512,768]{1,0:T(8,128)(2,1)S(1)} %get-tuple-element.11.rest_0_, bf16[1536,512]{1,0:T(8,128)(2,1)S(1)} %get-tuple-element.12.rest_1_, ...), custom_call_target="tpu_custom_call" | custom-call | flops 12884901 | bytes 4194 | tf_op jit(solution)/shard_map/conv/pallas_call | solution.py:443
  108.5 1.4 copy-done.3
  110.0 19.1 %collective-permute-done.refs_3_ = bf16[3,8,512]{2,1,0:T(8,128)(2,1)S(1)} collective-permute-done((bf16[3,8,512]{2,1,0:T(8,128)(2,1)S(1)}, bf16[3,8,512]{2,1,0:T(8,128)(2,1)S(1)}, u32[]{:S(2)}, u32[]{:S(2)}) %collective-permute-start) | collective-permute-done | bytes 24608 | tf_op jit(solution)/shard_map/ppermute | solution.py:386
  129.0 87.7 %all-to-all-done.1.parts_ref = bf16[8,3,520,256]{3,2,1,0:T(8,128)(2,1)} async-done(((bf16[8,3,520,256]{3,2,1,0:T(8,128)(2,1)}), bf16[8,3,520,256]{3,2,1,0:T(8,128)(2,1)}, u32[]{:S(2)}, u32[]{:S(2)}) %all-to-all-start.1) | async-done | bytes 6389792 | tf_op jit(solution)/shard_map/all_to_all | solution.py:500
  216.7 3.8 all-to-all-start.4
  220.5 1.4 copy-done.1
  223.8 42.6 %conv.5 = bf16[8,2,520,256]{3,2,1,0:T(8,128)(2,1)} custom-call(s32[1]{0:T(128)} %bitcast.place_ref, bf16[8,3,520,256]{3,2,1,0:T(8,128)(2,1)} %all-to-all-done.1.parts_ref, f32[3,3,512]{2,1,0:T(4,128)S(1)} %copy-done.14, bf16[512,768]{1,0:T(8,128)(2,1)S(1)} %get-tuple-element.11.rest_0_, bf16[1536,512]{1,0:T(8,128)(2,1)S(1)} %copy-done.1, ...), custom_call_target="tpu_custom_call" | custom-call | flops 25769804 | bytes 8388 | tf_op jit(solution)/shard_map/conv/pallas_call | solution.py:443
  266.5 2.9 all-to-all-done.4.refs_6_.refs_7_
  269.4 4.8 %all-to-all-start.3 = ((bf16[8,2,520,256]{3,2,1,0:T(8,128)(2,1)}), bf16[8,2,520,256]{3,2,1,0:T(8,128)(2,1)}, u32[]{:S(2)}, u32[]{:S(2)}) async-start(bf16[8,2,520,256]{3,2,1,0:T(8,128)(2,1)} %conv.5), calls=%async_computation.3 | async-start | bytes 8519680 | tf_op jit(solution)/shard_map/all_to_all | solution.py:531
  274.2 1.4 copy-done.2
  277.5 21.6 %conv.4 = bf16[8,1,520,256]{3,2,1,0:T(8,128)(2,1)S(1)} custom-call(s32[1]{0:T(128)} %bitcast.place_ref, bf16[8,3,520,256]{3,2,1,0:T(8,128)(2,1)} %all-to-all-done.1.parts_ref, f32[3,3,512]{2,1,0:T(4,128)S(1)} %copy-done.14, bf16[512,768]{1,0:T(8,128)(2,1)S(1)} %get-tuple-element.11.rest_0_, bf16[1536,512]{1,0:T(8,128)(2,1)S(1)} %copy-done.2, ...), custom_call_target="tpu_custom_call" | custom-call | flops 12884901 | bytes 4194 | tf_op jit(solution)/shard_map/conv/pallas_call | solution.py:443
  300.5 67.6 %all-to-all-done.3.refs_6_.refs_7_ = bf16[8,2,520,256]{3,2,1,0:T(8,128)(2,1)} async-done(((bf16[8,2,520,256]{3,2,1,0:T(8,128)(2,1)}), bf16[8,2,520,256]{3,2,1,0:T(8,128)(2,1)}, u32[]{:S(2)}, u32[]{:S(2)}) %all-to-all-start.3) | async-done | bytes 4259872 | tf_op jit(solution)/shard_map/all_to_all | solution.py:531
  368.0 4.3 %all-to-all-start.2 = ((bf16[8,1,520,256]{3,2,1,0:T(8,128)(2,1)}), bf16[8,1,520,256]{3,2,1,0:T(8,128)(2,1)}, u32[]{:S(2)}, u32[]{:S(2)}) async-start(bf16[8,1,520,256]{3,2,1,0:T(8,128)(2,1)} %copy-done.4), calls=%async_computation.2 | async-start | bytes 4259840 | tf_op jit(solution)/shard_map/all_to_all | solution.py:531
  372.4 8.7 %post.3.refs_8_ = f32[8192,512]{1,0:T(8,128)} custom-call(bf16[8192,512]{1,0:T(8,128)(2,1)} %refs_0_.6, bf16[8192,512]{1,0:T(8,128)(2,1)} %refs_1_.6, bf16[8192,512]{1,0:T(8,128)(2,1)} %refs_2_.6, bf16[3,8,512]{2,1,0:T(8,128)(2,1)S(1)} %collective-permute-done.refs_3_, f32[3,3,512]{2,1,0:T(4,128)S(1)} %copy-done.14, f32[1,512]{1,0:T(1,128)S(1)} %bitcast.8, ...), custom_call_target="tpu_custom_call" | custom-call | flops 62914 | bytes 12582 | tf_op jit(solution)/shard_map/post/pallas_call | solution.py:484
  381.1 16.0 %post.4.refs_8_ = f32[8192,512]{1,0:T(8,128)} custom-call(bf16[8192,512]{1,0:T(8,128)(2,1)} %refs_0_.6, bf16[8192,512]{1,0:T(8,128)(2,1)} %refs_1_.6, bf16[8192,512]{1,0:T(8,128)(2,1)} %refs_2_.6, bf16[3,8,512]{2,1,0:T(8,128)(2,1)S(1)} %collective-permute-done.refs_3_, f32[3,3,512]{2,1,0:T(4,128)S(1)} %copy-done.14, ...), custom_call_target="tpu_custom_call", output_to_operand_aliasing={{}: (8, {})} | custom-call | flops 125829 | bytes 25165 | tf_op jit(solution)/shard_map/post/pallas_call | solution.py:484
  397.1 23.6 %all-to-all-done.2.refs_6_.refs_7_ = bf16[8,1,520,256]{3,2,1,0:T(8,128)(2,1)} async-done(((bf16[8,1,520,256]{3,2,1,0:T(8,128)(2,1)}), bf16[8,1,520,256]{3,2,1,0:T(8,128)(2,1)}, u32[]{:S(2)}, u32[]{:S(2)}) %all-to-all-start.2) | async-done | bytes 2129952 | tf_op jit(solution)/shard_map/all_to_all | solution.py:531
  420.7 9.1 %post.5 = f32[8192,512]{1,0:T(8,128)} custom-call(bf16[8192,512]{1,0:T(8,128)(2,1)} %refs_0_.6, bf16[8192,512]{1,0:T(8,128)(2,1)} %refs_1_.6, bf16[8192,512]{1,0:T(8,128)(2,1)} %refs_2_.6, bf16[3,8,512]{2,1,0:T(8,128)(2,1)S(1)} %collective-permute-done.refs_3_, f32[3,3,512]{2,1,0:T(4,128)S(1)} %copy-done.14, ...), custom_call_target="tpu_custom_call", output_to_operand_aliasing={{}: (8, {})} | custom-call | flops 62914 | bytes 12582 | tf_op jit(solution)/shard_map/post/pallas_call | solution.py:484
  (42 shorter events, 9.3 us)
Async XLA Ops:
  1.5 16.4 %copy-start.14 = (f32[3,3,512]{2,1,0:T(4,128)S(1)}, f32[3,3,512]{2,1,0:T(4,128)}, u32[]{:S(2)}) copy-start(f32[3,3,512]{2,1,0:T(4,128)} %refs_4_.6) | copy-start | bytes 55300
  10.6 61.9 %all-to-all-start = ((bf16[8,1,584,256]{3,2,1,0:T(8,128)(2,1)}), bf16[8,1,584,256]{3,2,1,0:T(8,128)(2,1)}, u32[]{:S(2)}, u32[]{:S(2)}) async-start(bf16[8,1,584,256]{3,2,1,0:T(8,128)(2,1)} %pre.2), calls=%async_computation | async-start | bytes 4784128 | tf_op jit(solution)/shard_map/all_to_all | solution.py:498
  37.9 44.7 %copy-start.5 = (f32[256,256]{1,0:T(8,128)S(1)}, f32[256,256]{1,0:T(8,128)}, u32[]{:S(2)}) copy-start(f32[256,256]{1,0:T(8,128)} %constant.21.clone.refs_5_.rest_3_) | copy-start | bytes 786436
  37.9 44.7 %copy-start.6 = (f32[256,256]{1,0:T(8,128)S(1)}, f32[256,256]{1,0:T(8,128)}, u32[]{:S(2)}) copy-start(f32[256,256]{1,0:T(8,128)} %constant.20.clone.refs_4_.rest_2_) | copy-start | bytes 786436
  37.9 44.7 %copy-start.15 = (bf16[256,256]{1,0:T(8,128)(2,1)S(1)}, bf16[256,256]{1,0:T(8,128)(2,1)}, u32[]{:S(2)}) copy-start(bf16[256,256]{1,0:T(8,128)(2,1)} %constant.19.clone.refs_3_) | copy-start | bytes 393220
  37.9 44.7 %copy-start.16 = (bf16[256,256]{1,0:T(8,128)(2,1)S(1)}, bf16[256,256]{1,0:T(8,128)(2,1)}, u32[]{:S(2)}) copy-start(bf16[256,256]{1,0:T(8,128)(2,1)} %constant.18.clone.refs_2_) | copy-start | bytes 393220
  37.9 44.7 %copy-start.17 = (bf16[256,256]{1,0:T(8,128)(2,1)S(1)}, bf16[256,256]{1,0:T(8,128)(2,1)}, u32[]{:S(2)}) copy-start(bf16[256,256]{1,0:T(8,128)(2,1)} %constant.17.clone.refs_1_) | copy-start | bytes 393220
  37.9 44.7 %copy-start.18 = (bf16[256,256]{1,0:T(8,128)(2,1)S(1)}, bf16[256,256]{1,0:T(8,128)(2,1)}, u32[]{:S(2)}) copy-start(bf16[256,256]{1,0:T(8,128)(2,1)} %constant.16.clone.refs_0_) | copy-start | bytes 393220
  72.5 144.2 %all-to-all-start.1 = ((bf16[8,3,520,256]{3,2,1,0:T(8,128)(2,1)}), bf16[8,3,520,256]{3,2,1,0:T(8,128)(2,1)}, u32[]{:S(2)}, u32[]{:S(2)}) async-start(bf16[8,3,520,256]{3,2,1,0:T(8,128)(2,1)} %pre.3), calls=%async_computation.1 | async-start | bytes 12779520 | tf_op jit(solution)/shard_map/all_to_all | solution.py:500
  78.7 50.3 %collective-permute-start = (bf16[3,8,512]{2,1,0:T(8,128)(2,1)S(1)}, bf16[3,8,512]{2,1,0:T(8,128)(2,1)S(1)}, u32[]{:S(2)}, u32[]{:S(2)}) collective-permute-start(bf16[3,8,512]{2,1,0:T(8,128)(2,1)S(1)} %pad_maximum_fusion), channel_id=1, source_target_pairs={{0,1},{1,2},{2,3},{3,4},{4,5},{5,6},{6,7},{8,9},{9,10},{10,11},{11... | collective-permute-start | bytes 73736 | tf_op jit(solution)/shard_map/ppermute | solution.py:386
  85.5 21.9 %copy-start.7 = (f32[256,256]{1,0:T(8,128)}, f32[256,256]{1,0:T(8,128)S(1)}, u32[]{:S(2)}) copy-start(f32[256,256]{1,0:T(8,128)S(1)} %get-tuple-element.13.rest_4_) | copy-start | bytes 786436
  85.5 21.9 %copy-start.10 = (f32[256,256]{1,0:T(8,128)}, f32[256,256]{1,0:T(8,128)S(1)}, u32[]{:S(2)}) copy-start(f32[256,256]{1,0:T(8,128)S(1)} %get-tuple-element.14.rest_5_) | copy-start | bytes 786436
  107.4 1.2 copy-start
  108.5 1.4 copy-start.3
  216.7 52.7 %all-to-all-start.4 = ((bf16[8,1,520,256]{3,2,1,0:T(8,128)(2,1)}), bf16[8,1,520,256]{3,2,1,0:T(8,128)(2,1)S(1)}, u32[]{:S(2)}, u32[]{:S(2)}) async-start(bf16[8,1,520,256]{3,2,1,0:T(8,128)(2,1)} %copy-done.3), calls=%async_computation.4 | async-start | bytes 4259840 | tf_op jit(solution)/shard_map/all_to_all | solution.py:531
  220.5 1.4 copy-start.1
  221.9 0.9 copy-start.8
  222.9 0.9 copy-start.11
  269.4 98.6 %all-to-all-start.3 = ((bf16[8,2,520,256]{3,2,1,0:T(8,128)(2,1)}), bf16[8,2,520,256]{3,2,1,0:T(8,128)(2,1)}, u32[]{:S(2)}, u32[]{:S(2)}) async-start(bf16[8,2,520,256]{3,2,1,0:T(8,128)(2,1)} %conv.5), calls=%async_computation.3 | async-start | bytes 8519680 | tf_op jit(solution)/shard_map/all_to_all | solution.py:531
  274.2 1.4 copy-start.2
  275.6 0.9 copy-start.9
  277.5 94.9 %copy-start.20 = (f32[512]{0:T(512)S(1)}, f32[512]{0:T(512)}, u32[]{:S(2)}) copy-start(f32[512]{0:T(512)} %param.16) | copy-start | bytes 6148
  299.1 1.3 copy-start.4
  368.0 52.7 %all-to-all-start.2 = ((bf16[8,1,520,256]{3,2,1,0:T(8,128)(2,1)}), bf16[8,1,520,256]{3,2,1,0:T(8,128)(2,1)}, u32[]{:S(2)}, u32[]{:S(2)}) async-start(bf16[8,1,520,256]{3,2,1,0:T(8,128)(2,1)} %copy-done.4), calls=%async_computation.2 | async-start | bytes 4259840 | tf_op jit(solution)/shard_map/all_to_all | solution.py:531
  (3 other events, 2.4 us)
